TPU v7x, 768 devices: a whole 4x8x12 slice. The times are simulated.
768 devices in a mesh: row: 48 (over y_lo, z), col: 16 (over y_hi, x, core).
Axes of the slice: x: 4, y: 8 (y_hi: 2, y_lo: 4; y = y_hi * 4 + y_lo), z: 12, core: 2. Of those that a mesh axis runs over, the one named last changes fastest.
Arguments:
- object_field: float32 [2, 18432, 4096], P(None, 'row', 'col'), may hold values from -3 to 3
- probe_field: float32 [2, 256, 256], replicated, may hold values from -6 to 6
- amplitudes: bfloat16 [48, 16, 4, 256, 256], P('row', 'col'), may hold values from 0.5 to 16
- pos_rows: int32 [48, 16, 4], P('row', 'col'), may hold values from 0 to 383
- pos_cols: int32 [48, 16, 4], P('row', 'col'), may hold values from 0 to 255
- scan_pick: int32 [48, 16, 2], P('row', 'col'), may hold values from 0 to 3
- scan_count: int32 [768], P(('row', 'col')), may hold values from 1 to 2, 1152 in all
Outputs:
- object_next: float32 [2, 18432, 4096], P(None, 'row', 'col')
- probe_next: float32 [2, 256, 256], replicated
Inputs may be any that keep to these rules, and one draw needn't show every extreme that they name: `scan_count`: each tile's list has 1 to 2 scans; the longest list has exactly 2; lists total 1152 scans.
All inputs are finite; a program needn't handle non-finite values. No bound on the sum of `scan_count` on one device may be relied on, other than what follows from the above.
Results may differ from a plain program's by a relative error of at most 0.0003.
Values sent between devices are 32-bit elements; how exact they have to be, the bound alone decides.
No kernel may reach another device: no remote copies, remote signals or barrier semaphores. Data moves between devices by JAX's collectives and lax.ppermute only.
A program may use at most 64 MiB of HBM per device.

v0:
```python
import math

import jax
import jax.numpy as jnp
from jax import lax
from jax.sharding import PartitionSpec as P

PRECISE = lax.Precision.HIGHEST
SOFTENING = 0.25
OBJECT_REG = 0.5
PROBE_REG = 1.0


def passed_along(array, axis, by):
    peers = lax.axis_size(axis)
    pairs = [(i, i + by) for i in range(peers) if 0 <= i + by < peers]
    return lax.ppermute(array, axis, pairs)


def padded(array, sides, width):
    for axis, dim in sides:
        peers, length = (lax.axis_size(axis), array.shape[dim])
        up = [(i, (i + 1) % peers) for i in range(peers - 1)]
        down = [(j, i) for i, j in up]
        last = lax.slice_in_dim(array, length - width, length, axis=dim)
        first = lax.slice_in_dim(array, 0, width, axis=dim)
        before = lax.ppermute(last, axis, up)
        after = lax.ppermute(first, axis, down)
        array = jnp.concatenate([before, array, after], axis=dim)
    return array


def dft_tables(patch_width):
    grid_index = jnp.arange(patch_width, dtype=jnp.int32)
    phase_angle = (grid_index[:, None] * grid_index[None, :] % patch_width).astype(jnp.float32) * (
        2.0 * math.pi / patch_width
    )
    factor = 1.0 / math.sqrt(patch_width)
    return (jnp.cos(phase_angle) * factor, -jnp.sin(phase_angle) * factor)


def left_apply(table, data):
    return jnp.einsum("ka,sab->skb", table, data, precision=PRECISE)


def right_apply(data, table):
    return jnp.einsum("sab,bk->sak", data, table, precision=PRECISE)


def transform(real_part, imag_part, table_re, table_im):
    left_re = left_apply(table_re, real_part) - left_apply(table_im, imag_part)
    left_im = left_apply(table_re, imag_part) + left_apply(table_im, real_part)
    out_re = right_apply(left_re, table_re) - right_apply(left_im, table_im)
    out_im = right_apply(left_re, table_im) + right_apply(left_im, table_re)
    return (out_re, out_im)


def tile_terms(extended, probe_field, amps_tile, row_at, col_at, picks, count):
    patch_width = probe_field.shape[1]
    slot_count = picks.shape[0]
    table_re, table_im = dft_tables(patch_width)
    measured = amps_tile[picks].astype(jnp.float32)
    row_pick = row_at[picks]
    col_pick = col_at[picks]
    slot_live = (jnp.arange(slot_count, dtype=jnp.int32) < count).astype(jnp.float32)
    zero_idx = jnp.zeros((), jnp.int32)

    def cut_patch(row_start, col_start):
        return lax.dynamic_slice(
            extended, (zero_idx, row_start, col_start), (2, patch_width, patch_width)
        )

    patches = jax.vmap(cut_patch)(row_pick, col_pick)
    object_re = patches[:, 0]
    object_im = patches[:, 1]
    probe_re = probe_field[0]
    probe_im = probe_field[1]
    wave_re = probe_re * object_re - probe_im * object_im
    wave_im = probe_re * object_im + probe_im * object_re
    far_re, far_im = transform(wave_re, wave_im, table_re, table_im)
    modulus = jnp.sqrt(far_re * far_re + far_im * far_im + SOFTENING)
    weight = (measured / modulus - 1.0) * slot_live[:, None, None]
    back_re, back_im = transform(far_re * weight, far_im * weight, table_re, -table_im)
    grad_re = probe_re * back_re + probe_im * back_im
    grad_im = probe_re * back_im - probe_im * back_re
    probe_grad_re = jnp.sum(object_re * back_re + object_im * back_im, axis=0)
    probe_grad_im = jnp.sum(object_re * back_im - object_im * back_re, axis=0)
    probe_light = jnp.sum(
        slot_live[:, None, None] * (object_re * object_re + object_im * object_im), axis=0
    )
    lamp_power = probe_re * probe_re + probe_im * probe_im
    pieces = jnp.stack([grad_re, grad_im, slot_live[:, None, None] * lamp_power[None]], axis=1)
    grad_ext = jnp.zeros((3,) + extended.shape[1:], jnp.float32)

    def place_patch(slot_idx, running_sum):
        corner_at = (zero_idx, row_pick[slot_idx], col_pick[slot_idx])
        current = lax.dynamic_slice(running_sum, corner_at, (3, patch_width, patch_width))
        return lax.dynamic_update_slice(running_sum, current + pieces[slot_idx], corner_at)

    grad_ext = lax.fori_loop(0, slot_count, place_patch, grad_ext)
    return (grad_ext, (probe_grad_re, probe_grad_im, probe_light))


def fold_cols(running_sum, rim_width):
    inner_len = running_sum.shape[2] - 2 * rim_width
    center_part = running_sum[:, :, rim_width : rim_width + inner_len]
    for step_by in (1, -1):
        edge_strip = (
            running_sum[:, :, rim_width + inner_len :]
            if step_by == 1
            else running_sum[:, :, :rim_width]
        )
        arrived = passed_along(edge_strip, "col", step_by)
        if step_by == 1:
            center_part = center_part.at[:, :, :rim_width].add(arrived)
        else:
            center_part = center_part.at[:, :, inner_len - rim_width :].add(arrived)
    return center_part


def fold_rows(running_sum, rim_width):
    inner_len = running_sum.shape[1] - 2 * rim_width
    center_part = running_sum[:, rim_width : rim_width + inner_len, :]
    for step_by in (1, -1):
        edge_strip = (
            running_sum[:, rim_width + inner_len :, :]
            if step_by == 1
            else running_sum[:, :rim_width, :]
        )
        arrived = passed_along(edge_strip, "row", step_by)
        if step_by == 1:
            center_part = center_part.at[:, :rim_width, :].add(arrived)
        else:
            center_part = center_part.at[:, inner_len - rim_width :, :].add(arrived)
    return center_part


def per_device(object_field, probe_field, amplitudes, pos_rows, pos_cols, scan_pick, scan_count):
    patch_width = probe_field.shape[1]
    rim_width = patch_width // 2
    extended = padded(object_field, (("row", 1), ("col", 2)), rim_width)
    grad_ext, probe_terms = tile_terms(
        extended,
        probe_field,
        amplitudes[0, 0],
        pos_rows[0, 0],
        pos_cols[0, 0],
        scan_pick[0, 0],
        scan_count[0],
    )
    inside = fold_rows(fold_cols(grad_ext, rim_width), rim_width)
    light_plane = inside[2]
    probe_sums = lax.psum((probe_terms[0], probe_terms[1], probe_terms[2]), ("row", "col"))
    object_next = object_field + inside[0:2] / (light_plane + OBJECT_REG)
    probe_next = probe_field + jnp.stack([probe_sums[0], probe_sums[1]]) / (
        probe_sums[2] + PROBE_REG
    )
    return (object_next, probe_next)


def solution(mesh):
    in_specs = (
        P(None, "row", "col"),
        P(),
        P("row", "col", None, None, None),
        P("row", "col", None),
        P("row", "col", None),
        P("row", "col", None),
        P(("row", "col")),
    )
    out_specs = (P(None, "row", "col"), P())
    return jax.shard_map(
        per_device, mesh=mesh, in_specs=in_specs, out_specs=out_specs, check_vma=False
    )
```

profile of v0, /device:TPU:1, one launch (start us, length us, event | category | flops | bytes accessed | tf_op | source)
XLA Modules:
  0.0 659.6 jit_solution(10698251529686929630)
XLA Ops:
  7.2 1.2 fusion.148
  8.4 1.3 collective-permute-start.1
  9.7 5.5 collective-permute-start
  15.8 1.3 gather_fusion.1
  18.6 1.1 copy-done.3
  19.7 6.3 collective-permute-start.2
  26.1 7.2 %collective-permute-start.3 = (f32[2,640,128]{2,1,0:T(8,128)S(1)}, f32[2,640,128]{2,1,0:T(8,128)}, u32[]{:S(2)}, u32[]{:S(2)}) collective-permute-start(f32[2,640,128]{2,1,0:T(8,128)S(1)} %get-tuple-element.204), channel_id=1, source_target_pairs={{1,0},{2,1},{3,2},{4,3},{5,4},{6,5},{7,6},{8,7},{9,8},{10,9},{11,1... | collective-permute-start | bytes 1966088 | tf_op jit(solution)/shard_map/ppermute | solution.py:28
  34.1 1.3 gather_fusion.2
  38.1 1.5 pad_maximum_fusion
  39.7 5.8 while.19
  40.3 2.3 bitcast_dynamic-update-slice_fusion.2
  43.2 2.2 bitcast_dynamic-update-slice_fusion.2
  45.5 3.2 fusion.42
  48.7 1.9 fusion.46
  50.6 1.9 fusion.3
  52.5 1.8 fusion.29
  54.4 1.8 fusion.44
  56.2 1.9 fusion.2
  58.1 10.5 %convolution_add_fusion.2 = f32[2,256,256]{2,1,0:T(8,128)S(1)} fusion(f32[2,256,256]{2,1,0:T(8,128)S(1)} %fusion.29, f32[2,256,256]{1,2,0:T(8,128)S(1)} %fusion.2), kind=kOutput, calls=%fused_computation.14 | convolution fusion | flops 403767296 | bytes 1572864 | tf_op jit(solution)/shard_map/sab,bk->sak/dot_general | solution.py:47
  68.6 1.8 convolution_subtract_fusion.2
  70.5 2.0 fusion.35
  72.5 2.0 fusion.39
  74.5 2.0 fusion.1
  76.5 1.9 fusion.24
  78.4 2.0 fusion.37
  80.4 2.0 fusion
  82.4 1.8 convolution_add_fusion
  84.3 3.0 fusion.10
  87.3 2.4 broadcast_in_dim.2
  89.7 31.6 %while.18 = (s32[]{:T(128)}, f32[3,640,512]{2,1,0:T(8,128)}, s32[2]{0:T(128)S(1)}, s32[2]{0:T(128)S(1)}, f32[2,3,256,256]{3,2,0,1:T(8,128)S(1)}, /*index=5*/s32[]{:T(128)}, s32[]{:T(128)}, s32[]{:T(128)}, s32[]{:T(128)}) while((s32[]{:T(128)}, f32[3,640,512]{2,1,0:T(8,128)}, s32[2]{0:T(128)S(1)}, s32[2]{0:T(128)S(1)}, ...), condition=%wide.region_1.2_spmd, body=%wide.region_0.1_spmd.sunk | while | flops 196616 | bytes 3932369 | solution.py:100
  94.8 1.6 bitcast_add_fusion.2
  96.4 8.8 %dynamic_update_slice.8 = f32[3,640,512]{2,1,0:T(8,128)} dynamic-update-slice(f32[3,640,512]{2,1,0:T(8,128)} %get-tuple-element.299, f32[3,256,256]{2,1,0:T(8,128)S(1)} %bitcast_add_fusion.2, s32[]{:T(128)} %constant.166.clone.1..sunk, s32[]{:T(128)S(6)} %select_n.162, s32[]{:T(128)S(6)} %select_n.163) | dynamic-update-slice | bytes 1572868 | tf_op jit(solution)/shard_map/while/body/eval_jaxpr/dynamic_update_slice | solution.py:98
  110.2 1.6 bitcast_add_fusion.2
  111.8 9.5 %dynamic_update_slice.8 = f32[3,640,512]{2,1,0:T(8,128)} dynamic-update-slice(f32[3,640,512]{2,1,0:T(8,128)} %get-tuple-element.299, f32[3,256,256]{2,1,0:T(8,128)S(1)} %bitcast_add_fusion.2, s32[]{:T(128)} %constant.166.clone.1..sunk, s32[]{:T(128)S(6)} %select_n.162, s32[]{:T(128)S(6)} %select_n.163) | dynamic-update-slice | bytes 1572868 | tf_op jit(solution)/shard_map/while/body/eval_jaxpr/dynamic_update_slice | solution.py:98
  121.3 3.1 fusion.145
  124.4 2.1 collective-permute-start.4
  126.5 3.2 collective-permute-start.5
  129.9 7.9 %collective-permute-done.4 = f32[3,640,128]{2,1,0:T(8,128)} collective-permute-done((f32[3,640,128]{2,1,0:T(8,128)}, f32[3,640,128]{2,1,0:T(8,128)}, u32[]{:S(2)}, u32[]{:S(2)}) %collective-permute-start.4) | collective-permute-done | bytes 983072 | tf_op jit(solution)/shard_map/ppermute | solution.py:17
  137.8 1.6 add_dynamic-update-slice_fusion
  139.5 2.7 collective-permute-done.5
  143.2 4.9 collective-permute-start.6
  148.1 491.3 %all-reduce.3.cloned.1.call-done = (f32[1,256,256]{2,1,0:T(8,128)}, f32[1,256,256]{2,1,0:T(8,128)}, f32[256,256]{1,0:T(8,128)}) async-done(((f32[1,256,256]{2,1,0:T(8,128)}, f32[1,256,256]{2,1,0:T(8,128)}, f32[256,256]{1,0:T(8,128)}), (f32[1,256,256]{2,1,0:T(8,128)}, f32[1,256,256]{2,1,0:T(8,128)}, f32[256,256]{1,0:T(8,128)})) %all-reduce.3.cloned.1.call-update) | async-done | bytes 786448 | tf_op jit(solution)/shard_map/psum | solution.py:153
  639.3 1.0 broadcast_add_fusion
  640.3 1.3 collective-permute-start.7
  641.6 1.9 fusion.6
  643.6 1.1 fusion.20
  644.7 6.5 collective-permute-done.7
  651.4 1.0 fusion.5
  (64 shorter events, 10.3 us)
Async XLA Ops:
  7.2 26.9 %copy-start = (bf16[1,1,4,256,256]{4,3,2,1,0:T(8,128)(2,1)S(1)}, bf16[1,1,4,256,256]{4,3,2,1,0:T(8,128)(2,1)}, u32[]{:S(2)}) copy-start(bf16[1,1,4,256,256]{4,3,2,1,0:T(8,128)(2,1)} %param.19) | copy-start | bytes 1572868
  7.2 11.3 %copy-start.5 = (f32[2,384,256]{2,1,0:T(8,128)S(1)}, f32[2,384,256]{2,1,0:T(8,128)}, u32[]{:S(2)}) copy-start(f32[2,384,256]{2,1,0:T(8,128)} %param.17) | copy-start | bytes 2359300
  7.2 9.9 %copy-start.1 = (s32[1,1,4]{2,1,0:T(1,128)S(1)}, s32[1,1,4]{2,1,0:T(1,128)}, u32[]{:S(2)}) copy-start(s32[1,1,4]{2,1,0:T(1,128)} %param.20) | copy-start | bytes 52
  7.2 632.1 %all-reduce.3.cloned.1.call-start = ((), (), s32[]{:S(2)}) async-start(), calls=%async_computation | async-start | bytes 1572864 | tf_op jit(solution)/shard_map/psum | solution.py:153
  8.4 10.1 %collective-permute-start.1 = (f32[2,128,256]{2,1,0:T(8,128)S(1)}, f32[2,128,256]{2,1,0:T(8,128)S(1)}, u32[]{:S(2)}, u32[]{:S(2)}) collective-permute-start(f32[2,128,256]{2,1,0:T(8,128)S(1)} %get-tuple-element.207), channel_id=1, source_target_pairs={{16,0},{32,16},{48,32},{64,48},{80,64},{96,80},{112,96},{128,112},... | collective-permute-start | bytes 786440 | tf_op jit(solution)/shard_map/ppermute | solution.py:28
  9.7 8.7 %collective-permute-start = (f32[2,128,256]{2,1,0:T(8,128)S(1)}, f32[2,128,256]{2,1,0:T(8,128)S(1)}, u32[]{:S(2)}, u32[]{:S(2)}) collective-permute-start(f32[2,128,256]{2,1,0:T(8,128)S(1)} %get-tuple-element.208), channel_id=1, source_target_pairs={{0,16},{16,32},{32,48},{48,64},{64,80},{80,96},{96,112},{112,128},... | collective-permute-start | bytes 786440 | tf_op jit(solution)/shard_map/ppermute | solution.py:27
  18.6 1.1 copy-start.3
  19.7 15.7 %copy-start.9 = (f32[2,256,256]{2,1,0:T(8,128)S(1)}, f32[2,256,256]{2,1,0:T(8,128)}, u32[]{:S(2)}) copy-start(f32[2,256,256]{2,1,0:T(8,128)} %param.18) | copy-start | bytes 1572868
  19.7 17.2 %collective-permute-start.2 = (f32[2,640,128]{2,1,0:T(8,128)S(1)}, f32[2,640,128]{2,1,0:T(8,128)S(1)}, u32[]{:S(2)}, u32[]{:S(2)}) collective-permute-start(f32[2,640,128]{2,1,0:T(8,128)S(1)} %get-tuple-element.203), channel_id=1, source_target_pairs={{0,1},{1,2},{2,3},{3,4},{4,5},{5,6},{6,7},{7,8},{8,9},{9,10},{10,1... | collective-permute-start | bytes 1966088 | tf_op jit(solution)/shard_map/ppermute | solution.py:27
  26.1 12.0 %collective-permute-start.3 = (f32[2,640,128]{2,1,0:T(8,128)S(1)}, f32[2,640,128]{2,1,0:T(8,128)}, u32[]{:S(2)}, u32[]{:S(2)}) collective-permute-start(f32[2,640,128]{2,1,0:T(8,128)S(1)} %get-tuple-element.204), channel_id=1, source_target_pairs={{1,0},{2,1},{3,2},{4,3},{5,4},{6,5},{7,6},{8,7},{9,8},{10,9},{11,1... | collective-permute-start | bytes 1966088 | tf_op jit(solution)/shard_map/ppermute | solution.py:28
  35.3 2.8 copy-start.4
  37.0 0.8 copy-start.12
  45.5 3.3 copy-start.7
  45.5 3.3 copy-start.8
  58.1 12.4 %copy-start.13 = (bf16[2,256,256]{2,1,0:T(8,128)(2,1)S(1)}, bf16[2,256,256]{2,1,0:T(8,128)(2,1)}, u32[]{:S(2)}) copy-start(bf16[2,256,256]{2,1,0:T(8,128)(2,1)} %gather_fusion.2) | copy-start | bytes 786436
  84.3 3.0 copy-start.11
  121.3 8.4 %copy-start.2 = (f32[3,640,512]{2,1,0:T(8,128)S(1)}, f32[3,640,512]{2,1,0:T(8,128)}, u32[]{:S(2)}) copy-start(f32[3,640,512]{2,1,0:T(8,128)} %get-tuple-element.144) | copy-start | bytes 11796484
  124.4 13.5 %collective-permute-start.4 = (f32[3,640,128]{2,1,0:T(8,128)}, f32[3,640,128]{2,1,0:T(8,128)}, u32[]{:S(2)}, u32[]{:S(2)}) collective-permute-start(f32[3,640,128]{2,1,0:T(8,128)} %get-tuple-element.198), channel_id=1, source_target_pairs={{0,1},{1,2},{2,3},{3,4},{4,5},{5,6},{6,7},{7,8},{8,9},{9,10},{10,1... | collective-permute-start | bytes 2949128 | tf_op jit(solution)/shard_map/ppermute | solution.py:17
  126.5 15.6 %collective-permute-start.5 = (f32[3,640,128]{2,1,0:T(8,128)}, f32[3,640,128]{2,1,0:T(8,128)S(1)}, u32[]{:S(2)}, u32[]{:S(2)}) collective-permute-start(f32[3,640,128]{2,1,0:T(8,128)} %get-tuple-element.197), channel_id=1, source_target_pairs={{1,0},{2,1},{3,2},{4,3},{5,4},{6,5},{7,6},{8,7},{9,8},{10,9},{11,1... | collective-permute-start | bytes 2949128 | tf_op jit(solution)/shard_map/ppermute | solution.py:17
  142.3 499.2 %copy-start.10 = (f32[2,256,256]{2,1,0:T(8,128)S(1)}, f32[2,256,256]{2,1,0:T(8,128)}, u32[]{:S(2)}) copy-start(f32[2,256,256]{2,1,0:T(8,128)} %param.18) | copy-start | bytes 1572868
  143.2 500.4 %collective-permute-start.6 = (f32[3,128,256]{2,1,0:T(8,128)}, f32[3,128,256]{2,1,0:T(8,128)}, u32[]{:S(2)}, u32[]{:S(2)}) collective-permute-start(f32[3,128,256]{2,1,0:T(8,128)} %get-tuple-element.200), channel_id=1, source_target_pairs={{0,16},{16,32},{32,48},{48,64},{64,80},{80,96},{96,112},{112,128},... | collective-permute-start | bytes 1179656 | tf_op jit(solution)/shard_map/ppermute | solution.py:17
  640.3 10.9 %collective-permute-start.7 = (f32[3,128,256]{2,1,0:T(8,128)S(1)}, f32[3,128,256]{2,1,0:T(8,128)S(1)}, u32[]{:S(2)}, u32[]{:S(2)}) collective-permute-start(f32[3,128,256]{2,1,0:T(8,128)S(1)} %get-tuple-element.199), channel_id=1, source_target_pairs={{16,0},{32,16},{48,32},{64,48},{80,64},{96,80},{112,96},{128,112},... | collective-permute-start | bytes 1179656 | tf_op jit(solution)/shard_map/ppermute | solution.py:17
  643.6 7.8 %copy-start.6 = (f32[2,384,256]{2,1,0:T(8,128)S(1)}, f32[2,384,256]{2,1,0:T(8,128)}, u32[]{:S(2)}) copy-start(f32[2,384,256]{2,1,0:T(8,128)} %param.17) | copy-start | bytes 2359300
Sparse Core Ops, SparseCore 0:
  130.1 509.2 all-reduce.2
where the time goes:
time: 672 us; the launch traced here: 660 us
  waiting for transfers between devices  509 us (76%)
  matrix products  41.6 us (6%)
  local copies, waits for them, and re-layouts  39.5 us (6%)
  starting transfers between devices  31.8 us (5%)
  between operations  15.5 us (2%)
  other arithmetic  14.1 us (2%)
  loops' own time  7.81 us (1%)
    psum x1, waiting for transfers between devices, per_device(): lax.psum((probe_terms[0], probe_terms[1], probe_terms[2]), ('row', 'col'))  491 us
    dot_general x8, matrix products, right_apply(): return jnp.einsum('sab,bk->sak', data, table, precision=PRECISE)  24.7 us
    dynamic_update_slice x2, local copies, waits for them, and re-layouts, place_patch(): lax.dynamic_update_slice(running_sum, current + pieces[slot_idx], corner_at)  18.3 us
    ppermute x4, waiting for transfers between devices, passed_along(): return lax.ppermute(array, axis, pairs)  17.1 us
    dot_general x8, matrix products, left_apply(): return jnp.einsum('ka,sab->skb', table, data, precision=PRECISE)  16.9 us
  transfers between devices with their start and end apart: 9, of which 6 were waited for; matrix products, arithmetic and copies ran while one was open for 2% of the time, Pallas kernels for 0%

commit v1 on v0

v1 whole, which is shorter than its diff:
```python
import math

import jax
import jax.numpy as jnp
import numpy as np
from jax import lax
from jax.experimental import pallas as pl
from jax.experimental.pallas import tpu as pltpu
from jax.sharding import Mesh
from jax.sharding import PartitionSpec as P

SOFTENING = 0.25
OBJECT_REG = 0.5
PROBE_REG = 1.0
F32, BF16 = jnp.float32, jnp.bfloat16
VMEM_LIMIT = 60 * 1024 * 1024


def half_tables(width):
    half = width // 2
    n = np.arange(half)
    tables = []
    for odd in (0, 1):
        turn = ((2 * n[:, None] + odd) * n[None, :]) % width * (2.0 * np.pi / width)
        c, s = np.cos(turn) / math.sqrt(width), np.sin(turn) / math.sqrt(width)
        tables.append(np.block([[c, s], [-s, c]]))
    tables += [tables[0].T, tables[1].T]
    full = jnp.asarray(np.stack(tables), F32)
    high = full.astype(BF16)
    low = (full - high.astype(F32)).astype(BF16)
    return high, low


def sorting_table(width):
    order = np.concatenate([np.arange(0, width, 2), np.arange(1, width, 2)])
    return jnp.asarray(np.eye(width, dtype=np.float32)[order], BF16)


def dot(a, b):
    return lax.dot_general(a, b, (((1,), (0,)), ((), ())), preferred_element_type=F32)


def halves(x):
    high = x.astype(BF16)
    return high, (x - high.astype(F32)).astype(BF16)


def data_by_table(data, high, low):
    dh, dl = halves(data)
    return dot(dh, high) + (dot(dl, high) + dot(dh, low))


def table_by_data(high, low, data):
    dh, dl = halves(data)
    return dot(high, dh) + (dot(high, dl) + dot(low, dh))


def amplitude_kernel(pick, amps, order, out):
    ordered_rows = dot(order[...], amps[0]).astype(BF16)
    out[0] = lax.dot_general(
        ordered_rows, order[...], (((1,), (1,)), ((), ())), preferred_element_type=F32
    ).astype(BF16)


def ordered_amplitudes(amps, picks):
    slots, width = picks.shape[0], amps.shape[-1]
    return pl.pallas_call(
        amplitude_kernel,
        grid_spec=pltpu.PrefetchScalarGridSpec(
            num_scalar_prefetch=1,
            grid=(slots,),
            in_specs=[
                pl.BlockSpec((1, width, width), lambda s, pick: (pick[s], 0, 0)),
                pl.BlockSpec((width, width), lambda s, pick: (0, 0)),
            ],
            out_specs=pl.BlockSpec((1, width, width), lambda s, pick: (s, 0, 0)),
        ),
        out_shape=jax.ShapeDtypeStruct((slots, width, width), BF16),
        name="amplitude_order",
    )(picks, amps, sorting_table(width))


def scan_kernel(
    pick, rows_at, cols_at, count,
    center, above, below, left, right, probe, amps, high, low,
    grad_left, grad_center, grad_right, sums,
    ext, grad,
):
    width = probe.shape[1]
    rim = width // 2
    tall, wide = ext.shape[1:]
    th, tw = center.shape[1:]
    slots = amps.shape[0]
    ext[:, 0:rim, rim : rim + tw] = above[...]
    ext[:, rim : rim + th, rim : rim + tw] = center[...]
    ext[:, rim + th :, rim : rim + tw] = below[...]
    ext[:, :, 0:rim] = left[...]
    ext[:, :, rim + tw :] = right[...]
    grad[...] = jnp.zeros_like(grad)
    pr, pi = probe[0], probe[1]
    power = pr * pr + pi * pi
    total = [jnp.zeros((width, width), F32) for _ in range(3)]
    for s in range(slots):
        j = pick[s]
        r, c = rows_at[j], cols_at[j]
        live = (s < count[0]).astype(F32)
        skew = lax.rem(r, 8)
        rows = pl.ds(pl.multiple_of(r - skew, 8), width + 8)
        up = lax.rem(width + 8 - skew, width + 8)
        back = lax.rem(wide - c, wide)

        def cut(plane):
            block = pltpu.roll(ext[plane, rows, :], back, 1)[:, :width]
            return pltpu.roll(block, up, 0)[:width]

        o_r, o_i = cut(0), cut(1)
        w_r, w_i = pr * o_r - pi * o_i, pr * o_i + pi * o_r
        even = jnp.concatenate([w_r[:rim] + w_r[rim:], w_i[:rim] + w_i[rim:]], axis=0)
        odd = jnp.concatenate([w_r[:rim] - w_r[rim:], w_i[:rim] - w_i[rim:]], axis=0)
        even = table_by_data(high[0], low[0], even)
        odd = table_by_data(high[1], low[1], odd)
        y_r = jnp.concatenate([even[:rim], odd[:rim]], axis=0)
        y_i = jnp.concatenate([even[rim:], odd[rim:]], axis=0)
        even = jnp.concatenate([y_r[:, :rim] + y_r[:, rim:], y_i[:, :rim] + y_i[:, rim:]], axis=1)
        odd = jnp.concatenate([y_r[:, :rim] - y_r[:, rim:], y_i[:, :rim] - y_i[:, rim:]], axis=1)
        even = data_by_table(even, high[2], low[2])
        odd = data_by_table(odd, high[3], low[3])
        m = amps[s].astype(F32)

        def weighted(z, m):
            re, im = z[:, :rim], z[:, rim:]
            weight = (m * lax.rsqrt(re * re + im * im + SOFTENING) - 1.0) * live
            return jnp.concatenate([re * weight, im * weight], axis=1)

        even = data_by_table(weighted(even, m[:, :rim]), high[0], low[0])
        odd = data_by_table(weighted(odd, m[:, rim:]), high[1], low[1])
        plus, minus = even + odd, even - odd
        y_r = jnp.concatenate([plus[:, :rim], minus[:, :rim]], axis=1)
        y_i = jnp.concatenate([plus[:, rim:], minus[:, rim:]], axis=1)
        even = table_by_data(high[2], low[2], jnp.concatenate([y_r[:rim], y_i[:rim]], axis=0))
        odd = table_by_data(high[3], low[3], jnp.concatenate([y_r[rim:], y_i[rim:]], axis=0))
        plus, minus = even + odd, even - odd
        d_r = jnp.concatenate([plus[:rim], minus[:rim]], axis=0)
        d_i = jnp.concatenate([plus[rim:], minus[rim:]], axis=0)
        total[0] += o_r * d_r + o_i * d_i
        total[1] += o_r * d_i - o_i * d_r
        total[2] += live * (o_r * o_r + o_i * o_i)
        pieces = (pr * d_r + pi * d_i, pr * d_i - pi * d_r, live * power)
        for plane, piece in enumerate(pieces):
            tail = jnp.zeros((8, width), F32)
            spread = pltpu.roll(jnp.concatenate([piece, tail], axis=0), skew, 0)
            spread = jnp.concatenate([spread, jnp.zeros((width + 8, wide - width), F32)], axis=1)
            grad[plane, rows, :] += pltpu.roll(spread, c, 1)
    parts, _, part = sums.shape[:3]
    for plane in range(3):
        for p in range(parts):
            sums[p, plane] = total[plane][p * part : (p + 1) * part]
    grad_left[...] = grad[:, :, 0:rim]
    grad_center[...] = grad[:, :, rim : rim + tw]
    grad_right[...] = grad[:, :, rim + tw :]


def scans(picks, rows_at, cols_at, count, center, above, below, left, right, probe, amps, parts):
    width = probe.shape[1]
    rim = width // 2
    th, tw = center.shape[1:]
    tall, wide = th + 2 * rim, tw + 2 * rim
    high, low = half_tables(width)
    smem = pl.BlockSpec(memory_space=pltpu.SMEM)
    vmem = pl.BlockSpec(memory_space=pltpu.VMEM)
    return pl.pallas_call(
        scan_kernel,
        in_specs=[smem] * 4 + [vmem] * 9,
        out_specs=[vmem] * 4,
        out_shape=[
            jax.ShapeDtypeStruct((3, tall, rim), F32),
            jax.ShapeDtypeStruct((3, tall, tw), F32),
            jax.ShapeDtypeStruct((3, tall, rim), F32),
            jax.ShapeDtypeStruct((parts, 3, width // parts, width), F32),
        ],
        scratch_shapes=[pltpu.VMEM((2, tall, wide), F32), pltpu.VMEM((3, tall, wide), F32)],
        compiler_params=pltpu.CompilerParams(vmem_limit_bytes=VMEM_LIMIT),
        name="scan_step",
    )(picks, rows_at, cols_at, count, center, above, below, left, right, probe, amps, high, low)


ROW = ("y_lo", "z")
COL = ("y_hi", "x", "core")
NEAR = ("x", "core")
FAR = ("y_lo", "z", "y_hi")
SPLIT = {"y_lo": 4, "z": 12, "y_hi": 2, "x": 4, "core": 2}


def neighbours(last, first, axis):
    peers = lax.axis_size(axis)
    up = [(i, i + 1) for i in range(peers - 1)]
    down = [(j, i) for i, j in up]
    return lax.ppermute(last, axis, up), lax.ppermute(first, axis, down)


def exchanged(array, axes):
    return lax.all_to_all(array, axes, 0, 0, tiled=True)


def to_all(array, axes):
    return exchanged(jnp.broadcast_to(array[None], (lax.axis_size(axes),) + array.shape), axes)


def probe_update(sums, probe_field):
    near, _, part, width = sums.shape
    mine = exchanged(sums, NEAR).sum(0)
    far = lax.axis_size(FAR)
    mine = exchanged(mine.reshape(far, -1, width), FAR).sum(0)
    mine = to_all(mine, FAR).reshape(3, part, width)
    old = lax.dynamic_slice_in_dim(probe_field, lax.axis_index(NEAR) * part, part, axis=1)
    new = to_all(old + mine[0:2] / (mine[2] + PROBE_REG), NEAR)
    return new.transpose(1, 0, 2, 3).reshape(probe_field.shape)


def per_device(object_field, probe_field, amplitudes, pos_rows, pos_cols, scan_pick, scan_count):
    width = probe_field.shape[1]
    rim = width // 2
    th, tw = object_field.shape[1:]
    picks = scan_pick[0, 0]
    above, below = neighbours(object_field[:, th - rim :], object_field[:, :rim], ROW)
    amps = ordered_amplitudes(amplitudes[0, 0], picks)

    def column(part):
        return jnp.concatenate([above[:, :, part], object_field[:, :, part], below[:, :, part]], axis=1)

    left, right = neighbours(column(slice(tw - rim, tw)), column(slice(0, rim)), COL)
    grad_left, grad, grad_right, sums = scans(
        picks, pos_rows[0, 0], pos_cols[0, 0], scan_count,
        object_field, above, below, left, right, probe_field, amps, lax.axis_size(NEAR),
    )
    from_left, from_right = neighbours(grad_right, grad_left, COL)
    grad = jnp.concatenate([grad[:, :, :rim] + from_left, grad[:, :, rim:] + from_right], axis=2)
    from_above, from_below = neighbours(grad[:, th + rim :], grad[:, :rim], ROW)
    grad = grad[:, rim : rim + th]
    grad = grad.at[:, :rim].add(from_above).at[:, th - rim :].add(from_below)
    object_next = object_field + grad[0:2] / (grad[2] + OBJECT_REG)
    return object_next, probe_update(sums, probe_field)


def solution(mesh):
    fine = Mesh(mesh.devices.reshape(tuple(SPLIT.values())), tuple(SPLIT))
    in_specs = (
        P(None, ROW, COL),
        P(),
        P(ROW, COL, None, None, None),
        P(ROW, COL, None),
        P(ROW, COL, None),
        P(ROW, COL, None),
        P(ROW + COL),
    )
    out_specs = (P(None, ROW, COL), P())
    return jax.shard_map(per_device, mesh=fine, in_specs=in_specs, out_specs=out_specs, check_vma=False)
```

time: 672 us -> 172 us (0.26); the launches traced: 660 us -> 171 us
  waiting for transfers between devices: 509 us -> 36.9 us
  matrix products: 41.6 us -> 0 us
  starting transfers between devices: 31.8 us -> 72.1 us
  blocking collectives: 0 us -> 32 us
  local copies, waits for them, and re-layouts: 39.5 us -> 9 us
  between operations: 15.5 us -> 1.51 us
  Pallas kernels: 0 us -> 12.8 us
  loops' own time: 7.81 us -> 0 us
  other arithmetic: 14.1 us -> 6.99 us
    psum x1 -> x0, waiting for transfers between devices: 491 us -> none  [per_device(): lax.psum((probe_terms[0], probe_terms[1], probe_terms[2]), ('row', 'col'))]
    all_to_all x0 -> x3, starting transfers between devices: none -> 44.5 us  [exchanged(): return lax.all_to_all(array, axes, 0, 0, tiled=True)]
    dot_general x16 -> x0, matrix products: 41.6 us -> none  [the longest x8 24.7 us: right_apply(): return jnp.einsum('sab,bk->sak', data, table, precision=PRECISE)]
    all_to_all x0 -> x1, blocking collectives: none -> 32 us  [exchanged(): return lax.all_to_all(array, axes, 0, 0, tiled=True)]
    all_to_all x0 -> x3, waiting for transfers between devices: none -> 24.6 us  [exchanged(): return lax.all_to_all(array, axes, 0, 0, tiled=True)]
    dynamic_update_slice x2 -> x0, local copies, waits for them, and re-layouts: 18.3 us -> none  [place_patch(): lax.dynamic_update_slice(running_sum, current + pieces[slot_idx], corner_at)]
    pallas_call x0 -> x2, Pallas kernels: none -> 12.8 us  [the longest x1 9.79 us: scans(): pl.pallas_call(scan_kernel, in_specs=[smem] * 4 + [vmem] * 9, out_specs=[...]
    gather x9 -> x0, local copies, waits for them, and re-layouts: 8.96 us -> none
  transfers between devices with their start and end apart: 9 -> 11, of which waited for: 6 -> 7; matrix products, arithmetic and copies ran while one was open for 2% -> 6% of each run, Pallas kernels for 0% -> 2%
where the time goes in v1:
time: 172 us; the launch traced here: 171 us
  starting transfers between devices  72.1 us (42%)
  waiting for transfers between devices  36.9 us (21%)
  blocking collectives  32 us (19%)
  Pallas kernels  12.8 us (7%)
  local copies, waits for them, and re-layouts  9 us (5%)
  other arithmetic  6.99 us (4%)
    all_to_all x3, starting transfers between devices, exchanged(): return lax.all_to_all(array, axes, 0, 0, tiled=True)  44.5 us
    all_to_all x1, blocking collectives, exchanged(): return lax.all_to_all(array, axes, 0, 0, tiled=True)  32 us
    ppermute x8, starting transfers between devices, neighbours(): return (lax.ppermute(last, axis, up), lax.ppermute(first, axis, down))  27.5 us
    all_to_all x3, waiting for transfers between devices, exchanged(): return lax.all_to_all(array, axes, 0, 0, tiled=True)  24.6 us
    ppermute x8, waiting for transfers between devices, neighbours(): return (lax.ppermute(last, axis, up), lax.ppermute(first, axis, down))  12.3 us
    pallas_call x1, Pallas kernels, scans(): pl.pallas_call(scan_kernel, in_specs=[smem] * 4 + [vmem] * 9, out_specs=[...  9.79 us
  transfers between devices with their start and end apart: 11, of which 7 were waited for; matrix products, arithmetic and copies ran while one was open for 6% of the time, Pallas kernels for 2%

profile of v1, /device:TPU:1, one launch (start us, length us, event | category | flops | bytes accessed | tf_op | source)
XLA Modules:
  0.0 171.2 jit_solution(18220338978358930993)
XLA Ops:
  0.6 0.0 copy-start
  0.6 1.1 fusion.9
  1.8 4.8 %collective-permute-start = (f32[2,128,256]{2,1,0:T(8,128)S(1)}, f32[2,128,256]{2,1,0:T(8,128)S(1)}, u32[]{:S(2)}, u32[]{:S(2)}) collective-permute-start(f32[2,128,256]{2,1,0:T(8,128)S(1)} %get-tuple-element.41), channel_id=1, source_target_pairs={{0,16},{16,32},{32,48},{48,64},{64,80},{80,96},{96,112},{112,128},... | collective-permute-start | bytes 786440 | tf_op jit(solution)/shard_map/ppermute | solution.py:198
  6.6 1.3 collective-permute-start.1
  7.9 0.0 copy-done
  7.9 0.1 fusion.8
  8.0 1.9 %collective-permute-done.above = f32[2,128,256]{2,1,0:T(8,128)S(1)} collective-permute-done((f32[2,128,256]{2,1,0:T(8,128)S(1)}, f32[2,128,256]{2,1,0:T(8,128)S(1)}, u32[]{:S(2)}, u32[]{:S(2)}) %collective-permute-start) | collective-permute-done | bytes 262176 | tf_op jit(solution)/shard_map/ppermute | solution.py:198
  9.9 4.4 %collective-permute-done.1.below = f32[2,128,256]{2,1,0:T(8,128)S(1)} collective-permute-done((f32[2,128,256]{2,1,0:T(8,128)S(1)}, f32[2,128,256]{2,1,0:T(8,128)S(1)}, u32[]{:S(2)}, u32[]{:S(2)}) %collective-permute-start.1) | collective-permute-done | bytes 262176 | tf_op jit(solution)/shard_map/ppermute | solution.py:198
  14.5 9.4 %collective-permute-start.3 = (f32[2,640,128]{2,1,0:T(8,128)S(1)}, f32[2,640,128]{2,1,0:T(8,128)S(1)}, u32[]{:S(2)}, u32[]{:S(2)}) collective-permute-start(f32[2,640,128]{2,1,0:T(8,128)S(1)} %pad_maximum_fusion.1), channel_id=1, source_target_pairs={{1,0},{2,1},{3,2},{4,3},{5,4},{6,5},{7,6},{8,7},{9,8},{10,9},{11,1... | collective-permute-start | bytes 1966088 | tf_op jit(solution)/shard_map/ppermute | solution.py:198
  23.9 0.0 copy-done.3
  23.9 1.9 %collective-permute-start.2 = (f32[2,640,128]{2,1,0:T(8,128)S(1)}, f32[2,640,128]{2,1,0:T(8,128)S(1)}, u32[]{:S(2)}, u32[]{:S(2)}) collective-permute-start(f32[2,640,128]{2,1,0:T(8,128)S(1)} %pad_maximum_fusion), channel_id=1, source_target_pairs={{0,1},{1,2},{2,3},{3,4},{4,5},{5,6},{6,7},{7,8},{8,9},{9,10},{10,1... | collective-permute-start | bytes 1966088 | tf_op jit(solution)/shard_map/ppermute | solution.py:198
  26.5 3.0 %amplitude_order.1.amps = bf16[2,256,256]{2,1,0:T(8,128)(2,1)} custom-call(s32[2]{0:T(128)} %bitcast.17, bf16[4,256,256]{2,1,0:T(8,128)(2,1)} %bitcast.13, bf16[256,256]{1,0:T(8,128)(2,1)} %constant.79.clone.order), custom_call_target="tpu_custom_call" | custom-call | tf_op jit(solution)/shard_map/amplitude_order/pallas_call | solution.py:67
  29.5 0.0 collective-permute-done.3.right
  29.5 3.8 %collective-permute-done.2.left = f32[2,640,128]{2,1,0:T(8,128)S(1)} collective-permute-done((f32[2,640,128]{2,1,0:T(8,128)S(1)}, f32[2,640,128]{2,1,0:T(8,128)S(1)}, u32[]{:S(2)}, u32[]{:S(2)}) %collective-permute-start.2) | collective-permute-done | bytes 655392 | tf_op jit(solution)/shard_map/ppermute | solution.py:198
  33.3 0.8 copy-done.7
  34.2 9.8 %scan_step.1 = (f32[3,640,128]{2,1,0:T(8,128)}, f32[3,640,256]{2,1,0:T(8,128)}, f32[3,640,128]{2,1,0:T(8,128)}, f32[8,3,32,256]{3,2,1,0:T(8,128)}) custom-call(s32[2]{0:T(128)} %bitcast.18, s32[4]{0:T(128)} %bitcast.19, s32[4]{0:T(128)} %bitcast.20, s32[1]{0:T(128)S(6)} %copy.18.count, f32[2,384,256]{2,1,0:T(8,128)} %center.1, f32[2,128,256]{2,1,0:T(8,128)} %copy-done.2, ...), custom_call_target="tpu_custom_call" | custom-call | tf_op jit(solution)/shard_map/scan_step/pallas_call | solution.py:171
  44.0 4.4 %collective-permute-start.4 = (f32[3,640,128]{2,1,0:T(8,128)}, f32[3,640,128]{2,1,0:T(8,128)S(1)}, u32[]{:S(2)}, u32[]{:S(2)}) collective-permute-start(f32[3,640,128]{2,1,0:T(8,128)} %get-tuple-element.31), channel_id=1, source_target_pairs={{0,1},{1,2},{2,3},{3,4},{4,5},{5,6},{6,7},{7,8},{8,9},{9,10},{10,1... | collective-permute-start | bytes 2949128 | tf_op jit(solution)/shard_map/ppermute | solution.py:198
  48.4 1.9 %collective-permute-start.5 = (f32[3,640,128]{2,1,0:T(8,128)}, f32[3,640,128]{2,1,0:T(8,128)S(1)}, u32[]{:S(2)}, u32[]{:S(2)}) collective-permute-start(f32[3,640,128]{2,1,0:T(8,128)} %get-tuple-element.32), channel_id=1, source_target_pairs={{1,0},{2,1},{3,2},{4,3},{5,4},{6,5},{7,6},{8,7},{9,8},{10,9},{11,1... | collective-permute-start | bytes 2949128 | tf_op jit(solution)/shard_map/ppermute | solution.py:198
  50.3 32.0 %all_to_all.20 = f32[8,3,32,256]{3,2,1,0:T(8,128)S(1)} all-to-all(f32[8,3,32,256]{3,2,1,0:T(8,128)} %get-tuple-element.33), channel_id=1, replica_groups=mesh['y_lo'=4,'z'=12,'y_hi'=2,'x'=4,'core'=2] {'x','core'}, dimensions={0} | all-to-all | bytes 1572864 | tf_op jit(solution)/shard_map/all_to_all | solution.py:202
  82.3 0.1 reduce_sum.18
  82.4 0.7 reshape.87
  83.1 30.0 %all-to-all-start.1 = ((f32[96,1,256]{2,1,0:T(1,128)}), f32[96,1,256]{2,1,0:T(1,128)S(1)}, u32[]{:S(2)}, u32[]{:S(2)}) async-start(f32[96,1,256]{2,1,0:T(1,128)} %reshape.87), calls=%async_computation.1 | async-start | bytes 196608 | tf_op jit(solution)/shard_map/all_to_all | solution.py:202
  113.1 12.5 %all-to-all-done.1 = f32[96,1,256]{2,1,0:T(1,128)S(1)} async-done(((f32[96,1,256]{2,1,0:T(1,128)}), f32[96,1,256]{2,1,0:T(1,128)S(1)}, u32[]{:S(2)}, u32[]{:S(2)}) %all-to-all-start.1) | async-done | bytes 98336 | tf_op jit(solution)/shard_map/all_to_all | solution.py:202
  125.6 0.1 reduce_sum.19
  125.7 0.7 broadcast_in_dim.4
  126.4 6.9 %all-to-all-start.2 = ((f32[96,1,256]{2,1,0:T(1,128)}), f32[96,1,256]{2,1,0:T(1,128)}, u32[]{:S(2)}, u32[]{:S(2)}) async-start(f32[96,1,256]{2,1,0:T(1,128)} %broadcast_in_dim.4), calls=%async_computation.2 | async-start | bytes 196608 | tf_op jit(solution)/shard_map/all_to_all | solution.py:202
  133.3 0.0 collective-permute-done.4
  133.3 0.0 collective-permute-done.5
  133.3 0.9 copy-done.4
  134.3 0.9 copy-done.5
  135.2 2.3 %slice_add_fusion = (f32[3,640,128]{2,1,0:T(8,128)S(1)}, f32[3,640,128]{2,1,0:T(8,128)S(1)}) fusion(f32[3,640,128]{2,1,0:T(8,128)} %copy-done.5, f32[3,640,256]{2,1,0:T(8,128)} %get-tuple-element.30, f32[3,640,128]{2,1,0:T(8,128)} %copy-done.4), kind=kLoop, calls=%fused_computation.7 | loop fusion | flops 491520 | bytes 5898240 | tf_op jit(solution)/shard_map/add | solution.py:237
  137.5 0.8 fusion.2
  138.3 2.5 %collective-permute-start.6 = (f32[3,128,256]{2,1,0:T(8,128)}, f32[3,128,256]{2,1,0:T(8,128)S(1)}, u32[]{:S(2)}, u32[]{:S(2)}) collective-permute-start(f32[3,128,256]{2,1,0:T(8,128)} %fusion.2), channel_id=1, source_target_pairs={{0,16},{16,32},{32,48},{48,64},{64,80},{80,96},{96,112},{112,128},... | collective-permute-start | bytes 1179656 | tf_op jit(solution)/shard_map/ppermute | solution.py:198
  140.8 0.1 fusion
  140.9 4.7 %all-to-all-done.2 = f32[96,1,256]{2,1,0:T(1,128)} async-done(((f32[96,1,256]{2,1,0:T(1,128)}), f32[96,1,256]{2,1,0:T(1,128)}, u32[]{:S(2)}, u32[]{:S(2)}) %all-to-all-start.2) | async-done | bytes 98336 | tf_op jit(solution)/shard_map/all_to_all | solution.py:202
  145.6 0.8 slice.137
  146.5 0.8 slice_add_fusion.4
  147.3 0.9 divide_add_fusion
  148.1 0.8 broadcast_in_dim.5
  149.0 7.7 %all-to-all-start.3 = ((f32[8,2,32,256]{3,2,1,0:T(8,128)}), f32[8,2,32,256]{3,2,1,0:T(8,128)}, u32[]{:S(2)}, u32[]{:S(2)}) async-start(f32[8,2,32,256]{3,2,1,0:T(8,128)} %broadcast_in_dim.5), calls=%async_computation.3 | async-start | bytes 1048576 | tf_op jit(solution)/shard_map/all_to_all | solution.py:202
  156.6 0.0 collective-permute-done.6
  156.6 0.8 pad_maximum_fusion.2
  157.4 1.3 collective-permute-start.7
  158.7 7.4 %all-to-all-done.3 = f32[8,2,32,256]{3,2,1,0:T(8,128)} async-done(((f32[8,2,32,256]{3,2,1,0:T(8,128)}), f32[8,2,32,256]{3,2,1,0:T(8,128)}, u32[]{:S(2)}, u32[]{:S(2)}) %all-to-all-start.3) | async-done | bytes 524320 | tf_op jit(solution)/shard_map/all_to_all | solution.py:202
  166.1 1.9 %copy.11 = f32[8,2,32,256]{3,2,0,1:T(8,128)} copy(f32[8,2,32,256]{3,2,1,0:T(8,128)} %all-to-all-done.3) | data formatting | bytes 1048576 | tf_op jit(solution)/shard_map/all_to_all | solution.py:202
  168.0 2.1 %collective-permute-done.7 = f32[3,128,256]{2,1,0:T(8,128)S(1)} collective-permute-done((f32[3,128,256]{2,1,0:T(8,128)}, f32[3,128,256]{2,1,0:T(8,128)S(1)}, u32[]{:S(2)}, u32[]{:S(2)}) %collective-permute-start.7) | collective-permute-done | bytes 393248 | tf_op jit(solution)/shard_map/ppermute | solution.py:198
  170.1 0.1 fusion.7
  170.2 1.0 fusion.1
  (17 shorter events, 0.2 us)
Async XLA Ops:
  0.6 7.3 %copy-start = (f32[2,384,256]{2,1,0:T(8,128)S(1)}, f32[2,384,256]{2,1,0:T(8,128)}, u32[]{:S(2)}) copy-start(f32[2,384,256]{2,1,0:T(8,128)} %center.1) | copy-start | bytes 2359300
  1.8 8.1 %collective-permute-start = (f32[2,128,256]{2,1,0:T(8,128)S(1)}, f32[2,128,256]{2,1,0:T(8,128)S(1)}, u32[]{:S(2)}, u32[]{:S(2)}) collective-permute-start(f32[2,128,256]{2,1,0:T(8,128)S(1)} %get-tuple-element.41), channel_id=1, source_target_pairs={{0,16},{16,32},{32,48},{48,64},{64,80},{80,96},{96,112},{112,128},... | collective-permute-start | bytes 786440 | tf_op jit(solution)/shard_map/ppermute | solution.py:198
  6.6 7.7 %collective-permute-start.1 = (f32[2,128,256]{2,1,0:T(8,128)S(1)}, f32[2,128,256]{2,1,0:T(8,128)S(1)}, u32[]{:S(2)}, u32[]{:S(2)}) collective-permute-start(f32[2,128,256]{2,1,0:T(8,128)S(1)} %get-tuple-element.40), channel_id=1, source_target_pairs={{16,0},{32,16},{48,32},{64,48},{80,64},{96,80},{112,96},{128,112},... | collective-permute-start | bytes 786440 | tf_op jit(solution)/shard_map/ppermute | solution.py:198
  9.9 4.5 %copy-start.2 = (f32[2,128,256]{2,1,0:T(8,128)}, f32[2,128,256]{2,1,0:T(8,128)S(1)}, u32[]{:S(2)}) copy-start(f32[2,128,256]{2,1,0:T(8,128)S(1)} %collective-permute-done.above) | copy-start | bytes 786436
  14.4 9.5 %copy-start.3 = (f32[2,128,256]{2,1,0:T(8,128)}, f32[2,128,256]{2,1,0:T(8,128)S(1)}, u32[]{:S(2)}) copy-start(f32[2,128,256]{2,1,0:T(8,128)S(1)} %collective-permute-done.1.below) | copy-start | bytes 786436
  14.5 15.0 %collective-permute-start.3 = (f32[2,640,128]{2,1,0:T(8,128)S(1)}, f32[2,640,128]{2,1,0:T(8,128)S(1)}, u32[]{:S(2)}, u32[]{:S(2)}) collective-permute-start(f32[2,640,128]{2,1,0:T(8,128)S(1)} %pad_maximum_fusion.1), channel_id=1, source_target_pairs={{1,0},{2,1},{3,2},{4,3},{5,4},{6,5},{7,6},{8,7},{9,8},{10,9},{11,1... | collective-permute-start | bytes 1966088 | tf_op jit(solution)/shard_map/ppermute | solution.py:198
  23.9 9.4 %collective-permute-start.2 = (f32[2,640,128]{2,1,0:T(8,128)S(1)}, f32[2,640,128]{2,1,0:T(8,128)S(1)}, u32[]{:S(2)}, u32[]{:S(2)}) collective-permute-start(f32[2,640,128]{2,1,0:T(8,128)S(1)} %pad_maximum_fusion), channel_id=1, source_target_pairs={{0,1},{1,2},{2,3},{3,4},{4,5},{5,6},{6,7},{7,8},{8,9},{9,10},{10,1... | collective-permute-start | bytes 1966088 | tf_op jit(solution)/shard_map/ppermute | solution.py:198
  29.5 3.9 %copy-start.6 = (f32[2,640,128]{2,1,0:T(8,128)}, f32[2,640,128]{2,1,0:T(8,128)S(1)}, u32[]{:S(2)}) copy-start(f32[2,640,128]{2,1,0:T(8,128)S(1)} %collective-permute-done.3.right) | copy-start | bytes 1966084
  33.3 0.8 copy-start.7
  44.0 89.3 %collective-permute-start.4 = (f32[3,640,128]{2,1,0:T(8,128)}, f32[3,640,128]{2,1,0:T(8,128)S(1)}, u32[]{:S(2)}, u32[]{:S(2)}) collective-permute-start(f32[3,640,128]{2,1,0:T(8,128)} %get-tuple-element.31), channel_id=1, source_target_pairs={{0,1},{1,2},{2,3},{3,4},{4,5},{5,6},{6,7},{7,8},{8,9},{9,10},{10,1... | collective-permute-start | bytes 2949128 | tf_op jit(solution)/shard_map/ppermute | solution.py:198
  48.4 84.9 %collective-permute-start.5 = (f32[3,640,128]{2,1,0:T(8,128)}, f32[3,640,128]{2,1,0:T(8,128)S(1)}, u32[]{:S(2)}, u32[]{:S(2)}) collective-permute-start(f32[3,640,128]{2,1,0:T(8,128)} %get-tuple-element.32), channel_id=1, source_target_pairs={{1,0},{2,1},{3,2},{4,3},{5,4},{6,5},{7,6},{8,7},{9,8},{10,9},{11,1... | collective-permute-start | bytes 2949128 | tf_op jit(solution)/shard_map/ppermute | solution.py:198
  83.1 42.5 %all-to-all-start.1 = ((f32[96,1,256]{2,1,0:T(1,128)}), f32[96,1,256]{2,1,0:T(1,128)S(1)}, u32[]{:S(2)}, u32[]{:S(2)}) async-start(f32[96,1,256]{2,1,0:T(1,128)} %reshape.87), calls=%async_computation.1 | async-start | bytes 196608 | tf_op jit(solution)/shard_map/all_to_all | solution.py:202
  126.4 19.2 %all-to-all-start.2 = ((f32[96,1,256]{2,1,0:T(1,128)}), f32[96,1,256]{2,1,0:T(1,128)}, u32[]{:S(2)}, u32[]{:S(2)}) async-start(f32[96,1,256]{2,1,0:T(1,128)} %broadcast_in_dim.4), calls=%async_computation.2 | async-start | bytes 196608 | tf_op jit(solution)/shard_map/all_to_all | solution.py:202
  133.3 1.0 copy-start.4
  134.2 1.0 copy-start.5
  138.3 18.4 %collective-permute-start.6 = (f32[3,128,256]{2,1,0:T(8,128)}, f32[3,128,256]{2,1,0:T(8,128)S(1)}, u32[]{:S(2)}, u32[]{:S(2)}) collective-permute-start(f32[3,128,256]{2,1,0:T(8,128)} %fusion.2), channel_id=1, source_target_pairs={{0,16},{16,32},{32,48},{48,64},{64,80},{80,96},{96,112},{112,128},... | collective-permute-start | bytes 1179656 | tf_op jit(solution)/shard_map/ppermute | solution.py:198
  149.0 17.1 %all-to-all-start.3 = ((f32[8,2,32,256]{3,2,1,0:T(8,128)}), f32[8,2,32,256]{3,2,1,0:T(8,128)}, u32[]{:S(2)}, u32[]{:S(2)}) async-start(f32[8,2,32,256]{3,2,1,0:T(8,128)} %broadcast_in_dim.5), calls=%async_computation.3 | async-start | bytes 1048576 | tf_op jit(solution)/shard_map/all_to_all | solution.py:202
  157.4 12.6 %collective-permute-start.7 = (f32[3,128,256]{2,1,0:T(8,128)}, f32[3,128,256]{2,1,0:T(8,128)S(1)}, u32[]{:S(2)}, u32[]{:S(2)}) collective-permute-start(f32[3,128,256]{2,1,0:T(8,128)} %get-tuple-element.34), channel_id=1, source_target_pairs={{16,0},{32,16},{48,32},{64,48},{80,64},{96,80},{112,96},{128,112},... | collective-permute-start | bytes 1179656 | tf_op jit(solution)/shard_map/ppermute | solution.py:198
  168.0 2.2 %copy-start.1 = (f32[2,384,256]{2,1,0:T(8,128)S(1)}, f32[2,384,256]{2,1,0:T(8,128)}, u32[]{:S(2)}) copy-start(f32[2,384,256]{2,1,0:T(8,128)} %center.1) | copy-start | bytes 2359300

commit v2 on v1

--- a/solution.py
+++ b/solution.py
@@ -9,11 +9,15 @@
 from jax.sharding import Mesh
 from jax.sharding import PartitionSpec as P
 
+
 SOFTENING = 0.25
 OBJECT_REG = 0.5
 PROBE_REG = 1.0
 F32, BF16 = jnp.float32, jnp.bfloat16
-VMEM_LIMIT = 60 * 1024 * 1024
+VMEM_LIMIT = 24 * 1024 * 1024
+SMALL_VMEM = 10 * 1024 * 1024
+NOTE = 11
+TAIL = 8
 
 
 def half_tables(width):
@@ -76,29 +80,31 @@
             out_specs=pl.BlockSpec((1, width, width), lambda s, pick: (s, 0, 0)),
         ),
         out_shape=jax.ShapeDtypeStruct((slots, width, width), BF16),
+        compiler_params=pltpu.CompilerParams(vmem_limit_bytes=SMALL_VMEM),
         name="amplitude_order",
     )(picks, amps, sorting_table(width))
 
 
 def scan_kernel(
     pick, rows_at, cols_at, count,
-    center, above, below, left, right, probe, amps, high, low,
-    grad_left, grad_center, grad_right, sums,
+    center, above, below, left, right, corners_above, corners_below, probe, amps, high, low,
+    grad_above, grad_center, grad_below, sums,
     ext, grad,
 ):
     width = probe.shape[1]
     rim = width // 2
-    tall, wide = ext.shape[1:]
+    _, wide = ext.shape[1:]
     th, tw = center.shape[1:]
     slots = amps.shape[0]
-    ext[:, 0:rim, rim : rim + tw] = above[...]
     ext[:, rim : rim + th, rim : rim + tw] = center[...]
-    ext[:, rim + th :, rim : rim + tw] = below[...]
-    ext[:, :, 0:rim] = left[...]
-    ext[:, :, rim + tw :] = right[...]
+    for at, side, corners, skip in ((0, above, corners_above, 0), (rim + th, below, corners_below, TAIL)):
+        ext[:, at : at + rim, 0:rim] = corners[0:2, skip : skip + rim]
+        ext[:, at : at + rim, rim : rim + tw] = side[:, :rim]
+        ext[:, at : at + rim, rim + tw :] = corners[2:4, skip : skip + rim]
+    ext[:, rim : rim + th, 0:rim] = left[:, TAIL : TAIL + th]
+    ext[:, rim : rim + th, rim + tw :] = right[:, TAIL : TAIL + th]
     grad[...] = jnp.zeros_like(grad)
     pr, pi = probe[0], probe[1]
-    power = pr * pr + pi * pi
     total = [jnp.zeros((width, width), F32) for _ in range(3)]
     for s in range(slots):
         j = pick[s]
@@ -145,22 +151,24 @@
         total[0] += o_r * d_r + o_i * d_i
         total[1] += o_r * d_i - o_i * d_r
         total[2] += live * (o_r * o_r + o_i * o_i)
-        pieces = (pr * d_r + pi * d_i, pr * d_i - pi * d_r, live * power)
+        pieces = (pr * d_r + pi * d_i, pr * d_i - pi * d_r)
         for plane, piece in enumerate(pieces):
             tail = jnp.zeros((8, width), F32)
             spread = pltpu.roll(jnp.concatenate([piece, tail], axis=0), skew, 0)
             spread = jnp.concatenate([spread, jnp.zeros((width + 8, wide - width), F32)], axis=1)
             grad[plane, rows, :] += pltpu.roll(spread, c, 1)
-    parts, _, part = sums.shape[:3]
-    for plane in range(3):
-        for p in range(parts):
-            sums[p, plane] = total[plane][p * part : (p + 1) * part]
-    grad_left[...] = grad[:, :, 0:rim]
-    grad_center[...] = grad[:, :, rim : rim + tw]
-    grad_right[...] = grad[:, :, rim + tw :]
-
-
-def scans(picks, rows_at, cols_at, count, center, above, below, left, right, probe, amps, parts):
+    parts = sums.shape[0]
+    part = width // parts
+    for p in range(parts):
+        for q in range(6):
+            lanes = slice((q % 2) * rim, (q % 2 + 1) * rim)
+            sums[p, q * part : (q + 1) * part] = total[q // 2][p * part : (p + 1) * part, lanes]
+    grad_above[...] = grad[:, 0:rim]
+    grad_center[...] = grad[:, rim : rim + th]
+    grad_below[...] = grad[:, rim + th :]
+
+
+def scans(picks, rows_at, cols_at, count, center, edges, probe, amps, parts):
     width = probe.shape[1]
     rim = width // 2
     th, tw = center.shape[1:]
@@ -170,25 +178,112 @@
     vmem = pl.BlockSpec(memory_space=pltpu.VMEM)
     return pl.pallas_call(
         scan_kernel,
-        in_specs=[smem] * 4 + [vmem] * 9,
+        in_specs=[smem] * 4 + [vmem] * 11,
         out_specs=[vmem] * 4,
         out_shape=[
-            jax.ShapeDtypeStruct((3, tall, rim), F32),
-            jax.ShapeDtypeStruct((3, tall, tw), F32),
-            jax.ShapeDtypeStruct((3, tall, rim), F32),
-            jax.ShapeDtypeStruct((parts, 3, width // parts, width), F32),
+            jax.ShapeDtypeStruct((2, rim, wide), F32),
+            jax.ShapeDtypeStruct((2, th, wide), F32),
+            jax.ShapeDtypeStruct((2, rim, wide), F32),
+            jax.ShapeDtypeStruct((parts, 6 * width // parts, rim), F32),
         ],
-        scratch_shapes=[pltpu.VMEM((2, tall, wide), F32), pltpu.VMEM((3, tall, wide), F32)],
+        scratch_shapes=[pltpu.VMEM((2, tall, wide), F32), pltpu.VMEM((2, tall, wide), F32)],
         compiler_params=pltpu.CompilerParams(vmem_limit_bytes=VMEM_LIMIT),
         name="scan_step",
-    )(picks, rows_at, cols_at, count, center, above, below, left, right, probe, amps, high, low)
-
-
-ROW = ("y_lo", "z")
+    )(picks, rows_at, cols_at, count, center, *edges, probe, amps, high, low)
+
+
+def piece_kernel(index, sums, probe, out):
+    parts, rows, half = out.shape
+    part = rows // 4
+    at = pl.multiple_of(index[0] * part, part)
+    for q in range(4):
+        old = probe[q // 2, pl.ds(at, part), (q % 2) * half : (q % 2 + 1) * half]
+        grad, light = sums[q * part : (q + 1) * part], sums[(4 + q % 2) * part : (5 + q % 2) * part]
+        new = old + grad / (light + PROBE_REG)
+        for p in range(parts):
+            out[p, q * part : (q + 1) * part] = new
+
+
+def probe_piece(sums, probe, parts, index):
+    half = probe.shape[2] // 2
+    vmem = pl.BlockSpec(memory_space=pltpu.VMEM)
+    return pl.pallas_call(
+        piece_kernel,
+        in_specs=[pl.BlockSpec(memory_space=pltpu.SMEM), vmem, vmem],
+        out_specs=vmem,
+        out_shape=jax.ShapeDtypeStruct((parts, 4 * probe.shape[1] // parts, half), F32),
+        compiler_params=pltpu.CompilerParams(vmem_limit_bytes=SMALL_VMEM),
+        name="probe_piece",
+    )(index.astype(jnp.int32).reshape(1), sums, probe)
+
+
+def join_kernel(pieces, out):
+    parts, rows, half = pieces.shape
+    part = rows // 4
+    for p in range(parts):
+        for q in range(4):
+            lanes = slice((q % 2) * half, (q % 2 + 1) * half)
+            out[q // 2, p * part : (p + 1) * part, lanes] = pieces[p, q * part : (q + 1) * part]
+
+
+def probe_joined(pieces, probe):
+    vmem = pl.BlockSpec(memory_space=pltpu.VMEM)
+    return pl.pallas_call(
+        join_kernel,
+        in_specs=[vmem],
+        out_specs=vmem,
+        out_shape=jax.ShapeDtypeStruct(probe.shape, F32),
+        compiler_params=pltpu.CompilerParams(vmem_limit_bytes=SMALL_VMEM),
+        name="probe_join",
+    )(pieces)
+
+
+def light_kernel(scans_at, probe, share, lit):
+    width = probe.shape[1]
+    rim = width // 2
+    th, tw = share.shape
+    wide = tw + 2 * rim
+    lit[...] = jnp.zeros_like(lit)
+    power = probe[0] * probe[0] + probe[1] * probe[1]
+    power = jnp.concatenate([power, jnp.zeros((8, width), F32)], axis=0)
+    power = jnp.concatenate([power, jnp.zeros((width + 8, wide - width), F32)], axis=1)
+    for down in range(3):
+        for right in range(3):
+            for s in range(2):
+                base = NOTE * (3 * down + right)
+
+                @pl.when(s < scans_at[base + 10])
+                def _():
+                    j = base + scans_at[base + 8 + s]
+                    r, c = scans_at[j], scans_at[j + 4]
+                    skew = lax.rem(r, 8)
+                    rows = pl.ds(pl.multiple_of(r - skew + down * th, 8), width + 8)
+                    placed = pltpu.roll(pltpu.roll(power, skew, 0), c, 1)
+                    lit[rows, right * tw : right * tw + wide] += placed
+
+    share[...] = 1.0 / (lit[th + rim : 2 * th + rim, tw + rim : 2 * tw + rim] + OBJECT_REG)
+
+
+def light_share(scans_at, probe, th, tw):
+    width = probe.shape[1]
+    rim = width // 2
+    return pl.pallas_call(
+        light_kernel,
+        in_specs=[pl.BlockSpec(memory_space=pltpu.SMEM), pl.BlockSpec(memory_space=pltpu.VMEM)],
+        out_specs=pl.BlockSpec(memory_space=pltpu.VMEM),
+        out_shape=jax.ShapeDtypeStruct((th, tw), F32),
+        scratch_shapes=[pltpu.VMEM((3 * th + 2 * rim, 3 * tw + 2 * rim), F32)],
+        compiler_params=pltpu.CompilerParams(vmem_limit_bytes=SMALL_VMEM),
+        cost_estimate=pl.CostEstimate(flops=20_000_000, bytes_accessed=1_000_000, transcendentals=0),
+        name="light_share",
+    )(scans_at, probe)
+
+
+ROW = ("y_lo", "z_hi", "z_lo")
 COL = ("y_hi", "x", "core")
 NEAR = ("x", "core")
-FAR = ("y_lo", "z", "y_hi")
-SPLIT = {"y_lo": 4, "z": 12, "y_hi": 2, "x": 4, "core": 2}
+MID = ("y_lo", "y_hi")
+SPLIT = {"y_lo": 4, "z_hi": 3, "z_lo": 4, "y_hi": 2, "x": 4, "core": 2}
 
 
 def neighbours(last, first, axis):
@@ -199,47 +294,78 @@
 
 
 def exchanged(array, axes):
-    return lax.all_to_all(array, axes, 0, 0, tiled=True)
-
-
-def to_all(array, axes):
-    return exchanged(jnp.broadcast_to(array[None], (lax.axis_size(axes),) + array.shape), axes)
-
-
-def probe_update(sums, probe_field):
-    near, _, part, width = sums.shape
-    mine = exchanged(sums, NEAR).sum(0)
-    far = lax.axis_size(FAR)
-    mine = exchanged(mine.reshape(far, -1, width), FAR).sum(0)
-    mine = to_all(mine, FAR).reshape(3, part, width)
-    old = lax.dynamic_slice_in_dim(probe_field, lax.axis_index(NEAR) * part, part, axis=1)
-    new = to_all(old + mine[0:2] / (mine[2] + PROBE_REG), NEAR)
-    return new.transpose(1, 0, 2, 3).reshape(probe_field.shape)
+    return lax.all_to_all(array.reshape(lax.axis_size(axes), -1, array.shape[-1]), axes, 0, 0, tiled=True)
+
+
+def copied(array, axes):
+    return jnp.broadcast_to(array[None], (lax.axis_size(axes),) + array.shape)
+
+
+def halo(object_field, note):
+    rim = note.shape[0]
+    th, tw = object_field.shape[1:]
+    tail = jnp.broadcast_to(note, (2, TAIL, rim))
+    tail_wide = jnp.concatenate([tail] * (tw // rim), axis=2)
+
+    def column(part):
+        return jnp.concatenate([tail, object_field[:, :, part], tail], axis=1)
+
+    def line(part):
+        return jnp.concatenate([object_field[:, part], tail_wide], axis=1)
+
+    def corner(part):
+        return jnp.concatenate([left[:, part], right[:, part]], axis=0)
+
+    left, right = neighbours(column(slice(tw - rim, tw)), column(slice(0, rim)), COL)
+    above, below = neighbours(line(slice(th - rim, th)), line(slice(0, rim)), ROW)
+    corners_above, corners_below = neighbours(
+        corner(slice(TAIL + th - rim, TAIL + th + TAIL)), corner(slice(0, TAIL + rim)), ROW
+    )
+    notes = [
+        corners_above[0, rim, :NOTE], above[0, rim, :NOTE], corners_above[2, rim, :NOTE],
+        left[0, 0, :NOTE], note[:NOTE], right[0, 0, :NOTE],
+        corners_below[0, 0, :NOTE], below[0, rim, :NOTE], corners_below[2, 0, :NOTE],
+    ]
+    edges = (above, below, left, right, corners_above, corners_below)
+    return edges, jnp.concatenate(notes).astype(jnp.int32)
+
+
+def folded(grad, above, below):
+    rim = above.shape[1]
+    th = grad.shape[1]
+    from_above, from_below = neighbours(below, above, ROW)
+    grad = jnp.concatenate(
+        [grad[:, :rim] + from_above, grad[:, rim : th - rim], grad[:, th - rim :] + from_below], axis=1
+    )
+    from_left, from_right = neighbours(grad[:, :, -rim:], grad[:, :, :rim], COL)
+    grad = grad[:, :, rim:-rim]
+    return jnp.concatenate([grad[:, :, :rim] + from_left, grad[:, :, rim:] + from_right], axis=2)
 
 
 def per_device(object_field, probe_field, amplitudes, pos_rows, pos_cols, scan_pick, scan_count):
     width = probe_field.shape[1]
     rim = width // 2
     th, tw = object_field.shape[1:]
-    picks = scan_pick[0, 0]
-    above, below = neighbours(object_field[:, th - rim :], object_field[:, :rim], ROW)
+    picks, rows_at, cols_at = scan_pick[0, 0], pos_rows[0, 0], pos_cols[0, 0]
+    near = lax.axis_size(NEAR)
+    own = jnp.concatenate([rows_at, cols_at, picks, scan_count])
+    edges, scans_at = halo(object_field, jnp.pad(own.astype(F32), (0, rim - NOTE)))
     amps = ordered_amplitudes(amplitudes[0, 0], picks)
-
-    def column(part):
-        return jnp.concatenate([above[:, :, part], object_field[:, :, part], below[:, :, part]], axis=1)
-
-    left, right = neighbours(column(slice(tw - rim, tw)), column(slice(0, rim)), COL)
-    grad_left, grad, grad_right, sums = scans(
-        picks, pos_rows[0, 0], pos_cols[0, 0], scan_count,
-        object_field, above, below, left, right, probe_field, amps, lax.axis_size(NEAR),
+    above, grad, below, sums = scans(
+        picks, rows_at, cols_at, scan_count, object_field, edges, probe_field, amps, near
     )
-    from_left, from_right = neighbours(grad_right, grad_left, COL)
-    grad = jnp.concatenate([grad[:, :, :rim] + from_left, grad[:, :, rim:] + from_right], axis=2)
-    from_above, from_below = neighbours(grad[:, th + rim :], grad[:, :rim], ROW)
-    grad = grad[:, rim : rim + th]
-    grad = grad.at[:, :rim].add(from_above).at[:, th - rim :].add(from_below)
-    object_next = object_field + grad[0:2] / (grad[2] + OBJECT_REG)
-    return object_next, probe_update(sums, probe_field)
+    share = light_share(scans_at, probe_field, th, tw)
+    mine = exchanged(sums, NEAR).sum(0)
+    above, below, mine = lax.optimization_barrier((above, below, mine))
+    mine = exchanged(mine, MID)
+    share, mine = lax.optimization_barrier((share, mine))
+    grad = folded(grad, above, below)
+    mine = mine.sum(0)
+    mine = exchanged(copied(mine, ("z_lo",)), ("z_lo",)).sum(0)
+    mine = exchanged(copied(mine, ("z_hi",)), ("z_hi",)).sum(0)
+    mine = exchanged(copied(mine, MID), MID).reshape(-1, rim)
+    mine = exchanged(probe_piece(mine, probe_field, near, lax.axis_index(NEAR)), NEAR)
+    return object_field + grad * share, probe_joined(mine, probe_field)
 
 
 def solution(mesh):
@@ -254,4 +380,5 @@
         P(ROW + COL),
     )
     out_specs = (P(None, ROW, COL), P())
+
     return jax.shard_map(per_device, mesh=fine, in_specs=in_specs, out_specs=out_specs, check_vma=False)

time: 172 us -> 186 us (1.081)
  the two profiles are of different devices: /device:TPU:1 before, /device:TPU:15 now
where the time goes in v2:
time: 186 us; the launch traced here: 185 us
  starting transfers between devices  90.8 us (49%)
  waiting for transfers between devices  38 us (20%)
  blocking collectives  24.7 us (13%)
  Pallas kernels  13 us (7%)
  local copies, waits for them, and re-layouts  8.79 us (5%)
  other arithmetic  7.66 us (4%)
    ppermute x10, starting transfers between devices, neighbours(): return (lax.ppermute(last, axis, up), lax.ppermute(first, axis, down))  58.2 us
    all_to_all x4, starting transfers between devices, exchanged(): lax.all_to_all(array.reshape(lax.axis_size(axes), -1, array.shape[-1]), a...  32.6 us
    all_to_all x2, blocking collectives, exchanged(): lax.all_to_all(array.reshape(lax.axis_size(axes), -1, array.shape[-1]), a...  24.7 us
    ppermute x10, waiting for transfers between devices, neighbours(): return (lax.ppermute(last, axis, up), lax.ppermute(first, axis, down))  19.4 us
    all_to_all x4, waiting for transfers between devices, exchanged(): lax.all_to_all(array.reshape(lax.axis_size(axes), -1, array.shape[-1]), a...  18.6 us
    pallas_call x1, Pallas kernels, scans(): pl.pallas_call(scan_kernel, in_specs=[smem] * 4 + [vmem] * 11, out_specs=...  5.21 us
    pallas_call x1, Pallas kernels, light_share(): pl.pallas_call(light_kernel, in_specs=[pl.BlockSpec(memory_space=pltpu.SM...  4.85 us
  transfers between devices with their start and end apart: 14, of which 7 were waited for; matrix products, arithmetic and copies ran while one was open for 5% of the time, Pallas kernels for 4%

profile of v2, /device:TPU:15, one launch (start us, length us, event | category | flops | bytes accessed | tf_op | source)
XLA Modules:
  0.0 184.7 jit_solution(5766291143681817256)
XLA Ops:
  1.3 1.2 fusion.3
  2.6 0.1 add_convert_fusion
  2.7 0.1 pad_maximum_fusion.1
  2.8 7.0 %collective-permute-start.2 = (f32[2,400,128]{2,1,0:T(8,128)S(1)}, f32[2,400,128]{2,1,0:T(8,128)S(1)}, u32[]{:S(2)}, u32[]{:S(2)}) collective-permute-start(f32[2,400,128]{2,1,0:T(8,128)S(1)} %get-tuple-element.38), channel_id=1, source_target_pairs={{0,1},{1,2},{2,3},{3,4},{4,5},{5,6},{6,7},{7,8},{8,9},{9,10},{10,1... | collective-permute-start | bytes 1228808 | tf_op jit(solution)/shard_map/ppermute | solution.py:293
  9.8 1.9 %collective-permute-start.3 = (f32[2,400,128]{2,1,0:T(8,128)S(1)}, f32[2,400,128]{2,1,0:T(8,128)S(1)}, u32[]{:S(2)}, u32[]{:S(2)}) collective-permute-start(f32[2,400,128]{2,1,0:T(8,128)S(1)} %get-tuple-element.37), channel_id=1, source_target_pairs={{1,0},{2,1},{3,2},{4,3},{5,4},{6,5},{7,6},{8,7},{9,8},{10,9},{11,1... | collective-permute-start | bytes 1228808 | tf_op jit(solution)/shard_map/ppermute | solution.py:293
  11.9 15.2 %collective-permute-start.1 = (f32[2,136,256]{2,1,0:T(8,128)S(1)}, f32[2,136,256]{2,1,0:T(8,128)S(1)}, u32[]{:S(2)}, u32[]{:S(2)}) collective-permute-start(f32[2,136,256]{2,1,0:T(8,128)S(1)} %get-tuple-element.39), channel_id=1, source_target_pairs={{16,0},{32,16},{48,32},{64,48},{80,64},{96,80},{112,96},{128,112},... | collective-permute-start | bytes 835592 | tf_op jit(solution)/shard_map/ppermute | solution.py:293
  27.1 2.1 %collective-permute-start = (f32[2,136,256]{2,1,0:T(8,128)S(1)}, f32[2,136,256]{2,1,0:T(8,128)S(1)}, u32[]{:S(2)}, u32[]{:S(2)}) collective-permute-start(f32[2,136,256]{2,1,0:T(8,128)S(1)} %get-tuple-element.40), channel_id=1, source_target_pairs={{0,16},{16,32},{32,48},{48,64},{64,80},{80,96},{96,112},{112,128},... | collective-permute-start | bytes 835592 | tf_op jit(solution)/shard_map/ppermute | solution.py:293
  29.2 0.3 collective-permute-done.3.right
  29.5 10.8 %collective-permute-start.5 = (f32[4,136,128]{2,1,0:T(8,128)S(1)}, f32[4,136,128]{2,1,0:T(8,128)S(1)}, u32[]{:S(2)}, u32[]{:S(2)}) collective-permute-start(f32[4,136,128]{2,1,0:T(8,128)S(1)} %pad_maximum_fusion.7), channel_id=1, source_target_pairs={{16,0},{32,16},{48,32},{64,48},{80,64},{96,80},{112,96},{128,112},... | collective-permute-start | bytes 835592 | tf_op jit(solution)/shard_map/ppermute | solution.py:293
  40.4 1.9 %collective-permute-start.4 = (f32[4,136,128]{2,1,0:T(8,128)S(1)}, f32[4,136,128]{2,1,0:T(8,128)S(1)}, u32[]{:S(2)}, u32[]{:S(2)}) collective-permute-start(f32[4,136,128]{2,1,0:T(8,128)S(1)} %pad_maximum_fusion.6), channel_id=1, source_target_pairs={{0,16},{16,32},{32,48},{48,64},{64,80},{80,96},{96,112},{112,128},... | collective-permute-start | bytes 835592 | tf_op jit(solution)/shard_map/ppermute | solution.py:293
  42.3 1.2 amplitude_order.1.amps
  43.6 0.2 collective-permute-done.5.corners_below
  43.8 6.0 %collective-permute-done.4.corners_above = f32[4,136,128]{2,1,0:T(8,128)S(1)} collective-permute-done((f32[4,136,128]{2,1,0:T(8,128)S(1)}, f32[4,136,128]{2,1,0:T(8,128)S(1)}, u32[]{:S(2)}, u32[]{:S(2)}) %collective-permute-start.4) | collective-permute-done | bytes 278560 | tf_op jit(solution)/shard_map/ppermute | solution.py:293
  49.8 5.2 %scan_step.1 = (f32[2,128,512]{2,1,0:T(8,128)S(1)}, f32[2,384,512]{2,1,0:T(8,128)S(1)}, f32[2,128,512]{2,1,0:T(8,128)S(1)}, f32[8,192,128]{2,1,0:T(8,128)S(1)}) custom-call(s32[2]{0:T(128)S(1)} %bitcast.27, s32[4]{0:T(128)S(1)} %bitcast.29, s32[4]{0:T(128)S(1)} %bitcast.31, s32[1]{0:T(128)S(6)} %copy.11.count, f32[2,384,256]{2,1,0:T(8,128)S(1)} %copy-done, ...), custom_call_target="tpu_custom_call" | custom-call | tf_op jit(solution)/shard_map/scan_step/pallas_call | solution.py:179
  55.1 0.9 copy-done.3
  56.0 0.8 copy-done.15
  56.7 0.8 copy-done.16
  57.5 4.2 %all-to-all-start = ((f32[8,192,128]{2,1,0:T(8,128)}), f32[8,192,128]{2,1,0:T(8,128)}, u32[]{:S(2)}, u32[]{:S(2)}) async-start(f32[8,192,128]{2,1,0:T(8,128)} %copy-done.3), calls=%async_computation | async-start | bytes 1572864 | tf_op jit(solution)/shard_map/all_to_all | solution.py:297
  61.8 0.7 slice_bitcast_fusion.1
  62.4 0.7 slice_bitcast_fusion.6
  63.1 9.2 %all-to-all-done = f32[8,192,128]{2,1,0:T(8,128)} async-done(((f32[8,192,128]{2,1,0:T(8,128)}), f32[8,192,128]{2,1,0:T(8,128)}, u32[]{:S(2)}, u32[]{:S(2)}) %all-to-all-start) | async-done | bytes 786464 | tf_op jit(solution)/shard_map/all_to_all | solution.py:297
  72.4 1.8 reduce_sum.36
  74.2 1.9 %collective-permute-start.6 = (f32[2,128,512]{2,1,0:T(8,128)}, f32[2,128,512]{2,1,0:T(8,128)}, u32[]{:S(2)}, u32[]{:S(2)}) collective-permute-start(f32[2,128,512]{2,1,0:T(8,128)} %copy-done.16), channel_id=1, source_target_pairs={{0,16},{16,32},{32,48},{48,64},{64,80},{80,96},{96,112},{112,128},... | collective-permute-start | bytes 1572872 | tf_op jit(solution)/shard_map/ppermute | solution.py:293
  76.1 5.5 %collective-permute-start.7 = (f32[2,128,512]{2,1,0:T(8,128)}, f32[2,128,512]{2,1,0:T(8,128)}, u32[]{:S(2)}, u32[]{:S(2)}) collective-permute-start(f32[2,128,512]{2,1,0:T(8,128)} %copy-done.15), channel_id=1, source_target_pairs={{16,0},{32,16},{48,32},{64,48},{80,64},{96,80},{112,96},{128,112},... | collective-permute-start | bytes 1572872 | tf_op jit(solution)/shard_map/ppermute | solution.py:293
  81.6 0.7 slice_bitcast_fusion.3
  82.3 0.7 slice_bitcast_fusion
  82.9 17.6 %all-to-all-start.1 = ((f32[8,24,128]{2,1,0:T(8,128)}), f32[8,24,128]{2,1,0:T(8,128)S(1)}, u32[]{:S(2)}, u32[]{:S(2)}) async-start(f32[8,24,128]{2,1,0:T(8,128)} %bitcast.12), calls=%async_computation.1 | async-start | bytes 196608 | tf_op jit(solution)/shard_map/all_to_all | solution.py:297
  100.5 1.5 slice_add_fusion.1
  102.0 0.1 pad_maximum_fusion
  102.2 0.8 slice.101
  102.9 9.6 %collective-permute-start.8 = (f32[2,384,128]{2,1,0:T(8,128)}, f32[2,384,128]{2,1,0:T(8,128)}, u32[]{:S(2)}, u32[]{:S(2)}) collective-permute-start(f32[2,384,128]{2,1,0:T(8,128)} %slice.101), channel_id=1, source_target_pairs={{0,1},{1,2},{2,3},{3,4},{4,5},{5,6},{6,7},{7,8},{8,9},{9,10},{10,1... | collective-permute-start | bytes 1179656 | tf_op jit(solution)/shard_map/ppermute | solution.py:293
  112.5 0.7 slice_bitcast_fusion.5
  113.2 0.1 concatenate.43
  113.3 4.8 %light_share.1 = f32[384,256]{1,0:T(8,128)S(1)} custom-call(s32[99]{0:T(128)S(1)} %convert_element_type.21.scans_at, f32[2,256,256]{2,1,0:T(8,128)S(1)} %copy-done.1), custom_call_target="tpu_custom_call" | custom-call | flops 20000000 | bytes 1000000 | tf_op jit(solution)/shard_map/light_share/pallas_call | solution.py:270
  118.2 6.9 %all_to_all.30 = f32[4,24,128]{2,1,0:T(8,128)S(1)} all-to-all(f32[4,24,128]{2,1,0:T(8,128)S(1)} %broadcast_in_dim.9), channel_id=1, replica_groups=mesh['y_lo'=4,'z_hi'=3,'z_lo'=4,'y_hi'=2,'x'=4,'core'=2] {'z_lo'}, dimensions={0} | all-to-all | bytes 98304 | tf_op jit(solution)/shard_map/all_to_all | solution.py:297
  125.1 17.8 %all_to_all.31 = f32[3,24,128]{2,1,0:T(8,128)S(1)} all-to-all(f32[3,24,128]{2,1,0:T(8,128)S(1)} %broadcast_in_dim.10), channel_id=1, replica_groups=mesh['y_lo'=4,'z_hi'=3,'z_lo'=4,'y_hi'=2,'x'=4,'core'=2] {'z_hi'}, dimensions={0} | all-to-all | bytes 73728 | tf_op jit(solution)/shard_map/all_to_all | solution.py:297
  143.0 0.7 broadcast_in_dim.11
  143.6 3.3 %all-to-all-start.4 = ((f32[8,24,128]{2,1,0:T(8,128)}), f32[8,24,128]{2,1,0:T(8,128)S(1)}, u32[]{:S(2)}, u32[]{:S(2)}) async-start(f32[8,24,128]{2,1,0:T(8,128)} %broadcast_in_dim.11), calls=%async_computation.4 | async-start | bytes 196608 | tf_op jit(solution)/shard_map/all_to_all | solution.py:297
  146.9 6.0 %all-to-all-done.4 = f32[8,24,128]{2,1,0:T(8,128)S(1)} async-done(((f32[8,24,128]{2,1,0:T(8,128)}), f32[8,24,128]{2,1,0:T(8,128)S(1)}, u32[]{:S(2)}, u32[]{:S(2)}) %all-to-all-start.4) | async-done | bytes 98336 | tf_op jit(solution)/shard_map/all_to_all | solution.py:297
  152.9 0.9 probe_piece.1
  153.8 7.4 %all-to-all-start.5 = ((f32[8,128,128]{2,1,0:T(8,128)}), f32[8,128,128]{2,1,0:T(8,128)S(1)}, u32[]{:S(2)}, u32[]{:S(2)}) async-start(f32[8,128,128]{2,1,0:T(8,128)} %probe_piece.1), calls=%async_computation.5 | async-start | bytes 1048576 | tf_op jit(solution)/shard_map/all_to_all | solution.py:297
  161.2 1.9 %slice_add_fusion.3 = (f32[2,384,128]{2,1,0:T(8,128)}, f32[2,384,128]{2,1,0:T(8,128)}) fusion(f32[2,384,128]{2,1,0:T(8,128)} %collective-permute-done.8, f32[2,384,512]{2,1,0:T(8,128)S(1)} %pad_maximum_fusion), kind=kLoop, calls=%fused_computation.10 | loop fusion | flops 98304 | bytes 1966080 | tf_op jit(solution)/shard_map/add | solution.py:342
  163.1 2.3 %collective-permute-start.9 = (f32[2,384,128]{2,1,0:T(8,128)}, f32[2,384,128]{2,1,0:T(8,128)}, u32[]{:S(2)}, u32[]{:S(2)}) collective-permute-start(f32[2,384,128]{2,1,0:T(8,128)} %get-tuple-element.21), channel_id=1, source_target_pairs={{1,0},{2,1},{3,2},{4,3},{5,4},{6,5},{7,6},{8,7},{9,8},{10,9},{11,1... | collective-permute-start | bytes 1179656 | tf_op jit(solution)/shard_map/ppermute | solution.py:293
  165.4 3.4 %all-to-all-done.5.pieces = f32[8,128,128]{2,1,0:T(8,128)S(1)} async-done(((f32[8,128,128]{2,1,0:T(8,128)}), f32[8,128,128]{2,1,0:T(8,128)S(1)}, u32[]{:S(2)}, u32[]{:S(2)}) %all-to-all-start.5) | async-done | bytes 524320 | tf_op jit(solution)/shard_map/all_to_all | solution.py:297
  168.9 0.8 probe_join.1
  169.7 13.0 %collective-permute-done.9 = f32[2,384,128]{2,1,0:T(8,128)} collective-permute-done((f32[2,384,128]{2,1,0:T(8,128)}, f32[2,384,128]{2,1,0:T(8,128)}, u32[]{:S(2)}, u32[]{:S(2)}) %collective-permute-start.9) | collective-permute-done | bytes 393248 | tf_op jit(solution)/shard_map/ppermute | solution.py:293
  182.6 1.1 slice_add_fusion.2
  183.7 1.0 fusion
  (55 shorter events, 0.3 us)
Async XLA Ops:
  0.6 2.0 %copy-start.12 = (s32[1,1,2]{2,1,0:T(1,128)S(1)}, s32[1,1,2]{2,1,0:T(1,128)}, u32[]{:S(2)}) copy-start(s32[1,1,2]{2,1,0:T(1,128)} %param.14) | copy-start | bytes 28
  0.6 2.0 %copy-start.13 = (s32[1,1,4]{2,1,0:T(1,128)S(1)}, s32[1,1,4]{2,1,0:T(1,128)}, u32[]{:S(2)}) copy-start(s32[1,1,4]{2,1,0:T(1,128)} %param.12) | copy-start | bytes 52
  0.7 2.0 %copy-start.14 = (s32[1,1,4]{2,1,0:T(1,128)S(1)}, s32[1,1,4]{2,1,0:T(1,128)}, u32[]{:S(2)}) copy-start(s32[1,1,4]{2,1,0:T(1,128)} %param.13) | copy-start | bytes 52
  1.3 10.4 %copy-start = (f32[2,384,256]{2,1,0:T(8,128)S(1)}, f32[2,384,256]{2,1,0:T(8,128)}, u32[]{:S(2)}) copy-start(f32[2,384,256]{2,1,0:T(8,128)} %center.1) | copy-start | bytes 2359300
  2.8 26.4 %collective-permute-start.2 = (f32[2,400,128]{2,1,0:T(8,128)S(1)}, f32[2,400,128]{2,1,0:T(8,128)S(1)}, u32[]{:S(2)}, u32[]{:S(2)}) collective-permute-start(f32[2,400,128]{2,1,0:T(8,128)S(1)} %get-tuple-element.38), channel_id=1, source_target_pairs={{0,1},{1,2},{2,3},{3,4},{4,5},{5,6},{6,7},{7,8},{8,9},{9,10},{10,1... | collective-permute-start | bytes 1228808 | tf_op jit(solution)/shard_map/ppermute | solution.py:293
  9.8 19.7 %collective-permute-start.3 = (f32[2,400,128]{2,1,0:T(8,128)S(1)}, f32[2,400,128]{2,1,0:T(8,128)S(1)}, u32[]{:S(2)}, u32[]{:S(2)}) collective-permute-start(f32[2,400,128]{2,1,0:T(8,128)S(1)} %get-tuple-element.37), channel_id=1, source_target_pairs={{1,0},{2,1},{3,2},{4,3},{5,4},{6,5},{7,6},{8,7},{9,8},{10,9},{11,1... | collective-permute-start | bytes 1228808 | tf_op jit(solution)/shard_map/ppermute | solution.py:293
  11.8 30.5 %copy-start.4 = (bf16[1,1,4,256,256]{4,3,2,1,0:T(8,128)(2,1)S(1)}, bf16[1,1,4,256,256]{4,3,2,1,0:T(8,128)(2,1)}, u32[]{:S(2)}) copy-start(bf16[1,1,4,256,256]{4,3,2,1,0:T(8,128)(2,1)} %param.11) | copy-start | bytes 1572868
  11.8 30.5 %copy-start.11 = (bf16[256,256]{1,0:T(8,128)(2,1)S(1)}, bf16[256,256]{1,0:T(8,128)(2,1)}, u32[]{:S(2)}) copy-start(bf16[256,256]{1,0:T(8,128)(2,1)} %constant.18.clone.order) | copy-start | bytes 393220
  11.9 31.7 %collective-permute-start.1 = (f32[2,136,256]{2,1,0:T(8,128)S(1)}, f32[2,136,256]{2,1,0:T(8,128)S(1)}, u32[]{:S(2)}, u32[]{:S(2)}) collective-permute-start(f32[2,136,256]{2,1,0:T(8,128)S(1)} %get-tuple-element.39), channel_id=1, source_target_pairs={{16,0},{32,16},{48,32},{64,48},{80,64},{96,80},{112,96},{128,112},... | collective-permute-start | bytes 835592 | tf_op jit(solution)/shard_map/ppermute | solution.py:293
  27.1 22.7 %copy-start.1 = (f32[2,256,256]{2,1,0:T(8,128)S(1)}, f32[2,256,256]{2,1,0:T(8,128)}, u32[]{:S(2)}) copy-start(f32[2,256,256]{2,1,0:T(8,128)} %probe.5) | copy-start | bytes 1572868
  27.1 22.7 %copy-start.5 = (bf16[4,256,256]{2,1,0:T(8,128)(2,1)S(1)}, bf16[4,256,256]{2,1,0:T(8,128)(2,1)}, u32[]{:S(2)}) copy-start(bf16[4,256,256]{2,1,0:T(8,128)(2,1)} %constant.27.high) | copy-start | bytes 1572868
  27.1 22.7 %copy-start.6 = (bf16[4,256,256]{2,1,0:T(8,128)(2,1)S(1)}, bf16[4,256,256]{2,1,0:T(8,128)(2,1)}, u32[]{:S(2)}) copy-start(bf16[4,256,256]{2,1,0:T(8,128)(2,1)} %constant.30.low) | copy-start | bytes 1572868
  27.1 16.5 %collective-permute-start = (f32[2,136,256]{2,1,0:T(8,128)S(1)}, f32[2,136,256]{2,1,0:T(8,128)S(1)}, u32[]{:S(2)}, u32[]{:S(2)}) collective-permute-start(f32[2,136,256]{2,1,0:T(8,128)S(1)} %get-tuple-element.40), channel_id=1, source_target_pairs={{0,16},{16,32},{32,48},{48,64},{64,80},{80,96},{96,112},{112,128},... | collective-permute-start | bytes 835592 | tf_op jit(solution)/shard_map/ppermute | solution.py:293
  29.5 25.5 %copy-start.2 = (f32[2,400,128]{2,1,0:T(8,128)}, f32[2,400,128]{2,1,0:T(8,128)S(1)}, u32[]{:S(2)}) copy-start(f32[2,400,128]{2,1,0:T(8,128)S(1)} %collective-permute-done.3.right) | copy-start | bytes 1228804
  29.5 14.3 %collective-permute-start.5 = (f32[4,136,128]{2,1,0:T(8,128)S(1)}, f32[4,136,128]{2,1,0:T(8,128)S(1)}, u32[]{:S(2)}, u32[]{:S(2)}) collective-permute-start(f32[4,136,128]{2,1,0:T(8,128)S(1)} %pad_maximum_fusion.7), channel_id=1, source_target_pairs={{16,0},{32,16},{48,32},{64,48},{80,64},{96,80},{112,96},{128,112},... | collective-permute-start | bytes 835592 | tf_op jit(solution)/shard_map/ppermute | solution.py:293
  40.4 9.4 %collective-permute-start.4 = (f32[4,136,128]{2,1,0:T(8,128)S(1)}, f32[4,136,128]{2,1,0:T(8,128)S(1)}, u32[]{:S(2)}, u32[]{:S(2)}) collective-permute-start(f32[4,136,128]{2,1,0:T(8,128)S(1)} %pad_maximum_fusion.6), channel_id=1, source_target_pairs={{0,16},{16,32},{32,48},{48,64},{64,80},{80,96},{96,112},{112,128},... | collective-permute-start | bytes 835592 | tf_op jit(solution)/shard_map/ppermute | solution.py:293
  43.6 11.4 %copy-start.9 = (f32[2,136,256]{2,1,0:T(8,128)}, f32[2,136,256]{2,1,0:T(8,128)S(1)}, u32[]{:S(2)}) copy-start(f32[2,136,256]{2,1,0:T(8,128)S(1)} %collective-permute-done.1.below) | copy-start | bytes 835588
  43.6 11.4 %copy-start.10 = (f32[2,136,256]{2,1,0:T(8,128)}, f32[2,136,256]{2,1,0:T(8,128)S(1)}, u32[]{:S(2)}) copy-start(f32[2,136,256]{2,1,0:T(8,128)S(1)} %collective-permute-done.above) | copy-start | bytes 835588
  43.8 11.2 %copy-start.8 = (f32[4,136,128]{2,1,0:T(8,128)}, f32[4,136,128]{2,1,0:T(8,128)S(1)}, u32[]{:S(2)}) copy-start(f32[4,136,128]{2,1,0:T(8,128)S(1)} %collective-permute-done.5.corners_below) | copy-start | bytes 835588
  49.8 5.3 %copy-start.7 = (f32[4,136,128]{2,1,0:T(8,128)}, f32[4,136,128]{2,1,0:T(8,128)S(1)}, u32[]{:S(2)}) copy-start(f32[4,136,128]{2,1,0:T(8,128)S(1)} %collective-permute-done.4.corners_above) | copy-start | bytes 835588
  55.1 0.9 copy-start.3
  56.0 0.8 copy-start.15
  56.7 0.8 copy-start.16
  57.5 14.8 %all-to-all-start = ((f32[8,192,128]{2,1,0:T(8,128)}), f32[8,192,128]{2,1,0:T(8,128)}, u32[]{:S(2)}, u32[]{:S(2)}) async-start(f32[8,192,128]{2,1,0:T(8,128)} %copy-done.3), calls=%async_computation | async-start | bytes 1572864 | tf_op jit(solution)/shard_map/all_to_all | solution.py:297
  74.2 26.4 %collective-permute-start.6 = (f32[2,128,512]{2,1,0:T(8,128)}, f32[2,128,512]{2,1,0:T(8,128)}, u32[]{:S(2)}, u32[]{:S(2)}) collective-permute-start(f32[2,128,512]{2,1,0:T(8,128)} %copy-done.16), channel_id=1, source_target_pairs={{0,16},{16,32},{32,48},{48,64},{64,80},{80,96},{96,112},{112,128},... | collective-permute-start | bytes 1572872 | tf_op jit(solution)/shard_map/ppermute | solution.py:293
  76.1 24.4 %collective-permute-start.7 = (f32[2,128,512]{2,1,0:T(8,128)}, f32[2,128,512]{2,1,0:T(8,128)}, u32[]{:S(2)}, u32[]{:S(2)}) collective-permute-start(f32[2,128,512]{2,1,0:T(8,128)} %copy-done.15), channel_id=1, source_target_pairs={{16,0},{32,16},{48,32},{64,48},{80,64},{96,80},{112,96},{128,112},... | collective-permute-start | bytes 1572872 | tf_op jit(solution)/shard_map/ppermute | solution.py:293
  82.9 35.2 %all-to-all-start.1 = ((f32[8,24,128]{2,1,0:T(8,128)}), f32[8,24,128]{2,1,0:T(8,128)S(1)}, u32[]{:S(2)}, u32[]{:S(2)}) async-start(f32[8,24,128]{2,1,0:T(8,128)} %bitcast.12), calls=%async_computation.1 | async-start | bytes 196608 | tf_op jit(solution)/shard_map/all_to_all | solution.py:297
  102.9 58.3 %collective-permute-start.8 = (f32[2,384,128]{2,1,0:T(8,128)}, f32[2,384,128]{2,1,0:T(8,128)}, u32[]{:S(2)}, u32[]{:S(2)}) collective-permute-start(f32[2,384,128]{2,1,0:T(8,128)} %slice.101), channel_id=1, source_target_pairs={{0,1},{1,2},{2,3},{3,4},{4,5},{5,6},{6,7},{7,8},{8,9},{9,10},{10,1... | collective-permute-start | bytes 1179656 | tf_op jit(solution)/shard_map/ppermute | solution.py:293
  143.6 9.3 %all-to-all-start.4 = ((f32[8,24,128]{2,1,0:T(8,128)}), f32[8,24,128]{2,1,0:T(8,128)S(1)}, u32[]{:S(2)}, u32[]{:S(2)}) async-start(f32[8,24,128]{2,1,0:T(8,128)} %broadcast_in_dim.11), calls=%async_computation.4 | async-start | bytes 196608 | tf_op jit(solution)/shard_map/all_to_all | solution.py:297
  153.8 15.1 %all-to-all-start.5 = ((f32[8,128,128]{2,1,0:T(8,128)}), f32[8,128,128]{2,1,0:T(8,128)S(1)}, u32[]{:S(2)}, u32[]{:S(2)}) async-start(f32[8,128,128]{2,1,0:T(8,128)} %probe_piece.1), calls=%async_computation.5 | async-start | bytes 1048576 | tf_op jit(solution)/shard_map/all_to_all | solution.py:297
  163.1 19.5 %collective-permute-start.9 = (f32[2,384,128]{2,1,0:T(8,128)}, f32[2,384,128]{2,1,0:T(8,128)}, u32[]{:S(2)}, u32[]{:S(2)}) collective-permute-start(f32[2,384,128]{2,1,0:T(8,128)} %get-tuple-element.21), channel_id=1, source_target_pairs={{1,0},{2,1},{3,2},{4,3},{5,4},{6,5},{7,6},{8,7},{9,8},{10,9},{11,1... | collective-permute-start | bytes 1179656 | tf_op jit(solution)/shard_map/ppermute | solution.py:293
  168.9 14.9 %copy-start.17 = (f32[2,384,128]{2,1,0:T(8,128)S(1)}, f32[2,384,128]{2,1,0:T(8,128)}, u32[]{:S(2)}) copy-start(f32[2,384,128]{2,1,0:T(8,128)} %get-tuple-element.20) | copy-start | bytes 1179652

commit v3 on v2

--- a/solution.py
+++ b/solution.py
@@ -86,9 +86,9 @@
 
 
 def scan_kernel(
-    pick, rows_at, cols_at, count,
-    center, above, below, left, right, corners_above, corners_below, probe, amps, high, low,
-    grad_above, grad_center, grad_below, sums,
+    pick, rows_at, cols_at, count, odd,
+    center, col_a, col_b, row_a, row_b, probe, amps, high, low,
+    grad_a, grad_center, grad_b, sums,
     ext, grad,
 ):
     width = probe.shape[1]
@@ -96,13 +96,16 @@
     _, wide = ext.shape[1:]
     th, tw = center.shape[1:]
     slots = amps.shape[0]
-    ext[:, rim : rim + th, rim : rim + tw] = center[...]
-    for at, side, corners, skip in ((0, above, corners_above, 0), (rim + th, below, corners_below, TAIL)):
-        ext[:, at : at + rim, 0:rim] = corners[0:2, skip : skip + rim]
-        ext[:, at : at + rim, rim : rim + tw] = side[:, :rim]
-        ext[:, at : at + rim, rim + tw :] = corners[2:4, skip : skip + rim]
-    ext[:, rim : rim + th, 0:rim] = left[:, TAIL : TAIL + th]
-    ext[:, rim : rim + th, rim + tw :] = right[:, TAIL : TAIL + th]
+    foot, side = rim + th, rim + tw
+    lines = [pl.ds(pl.multiple_of(at, rim), rim) for at in (foot * (1 - odd[0]), foot * odd[0])]
+    lanes = [pl.ds(pl.multiple_of(at, rim), rim) for at in (side * (1 - odd[1]), side * odd[1])]
+    ext[:, rim:foot, rim:side] = center[...]
+    for line, row in zip(lines, (row_a, row_b)):
+        ext[:, line, rim:side] = row[:, :rim, rim:side]
+        ext[:, line, lanes[0]] = row[:, :rim, :rim]
+        ext[:, line, lanes[1]] = row[:, :rim, side:]
+    ext[:, rim:foot, lanes[0]] = col_a[:, :th]
+    ext[:, rim:foot, lanes[1]] = col_b[:, :th]
     grad[...] = jnp.zeros_like(grad)
     pr, pi = probe[0], probe[1]
     total = [jnp.zeros((width, width), F32) for _ in range(3)]
@@ -161,14 +164,14 @@
     part = width // parts
     for p in range(parts):
         for q in range(6):
-            lanes = slice((q % 2) * rim, (q % 2 + 1) * rim)
-            sums[p, q * part : (q + 1) * part] = total[q // 2][p * part : (p + 1) * part, lanes]
-    grad_above[...] = grad[:, 0:rim]
-    grad_center[...] = grad[:, rim : rim + th]
-    grad_below[...] = grad[:, rim + th :]
-
-
-def scans(picks, rows_at, cols_at, count, center, edges, probe, amps, parts):
+            half = slice((q % 2) * rim, (q % 2 + 1) * rim)
+            sums[p, q * part : (q + 1) * part] = total[q // 2][p * part : (p + 1) * part, half]
+    grad_a[...] = grad[:, lines[0]]
+    grad_center[...] = grad[:, rim:foot]
+    grad_b[...] = grad[:, lines[1]]
+
+
+def scans(picks, rows_at, cols_at, count, odd, center, edges, probe, amps, parts):
     width = probe.shape[1]
     rim = width // 2
     th, tw = center.shape[1:]
@@ -178,7 +181,7 @@
     vmem = pl.BlockSpec(memory_space=pltpu.VMEM)
     return pl.pallas_call(
         scan_kernel,
-        in_specs=[smem] * 4 + [vmem] * 11,
+        in_specs=[smem] * 5 + [vmem] * 9,
         out_specs=[vmem] * 4,
         out_shape=[
             jax.ShapeDtypeStruct((2, rim, wide), F32),
@@ -189,7 +192,7 @@
         scratch_shapes=[pltpu.VMEM((2, tall, wide), F32), pltpu.VMEM((2, tall, wide), F32)],
         compiler_params=pltpu.CompilerParams(vmem_limit_bytes=VMEM_LIMIT),
         name="scan_step",
-    )(picks, rows_at, cols_at, count, center, *edges, probe, amps, high, low)
+    )(picks, rows_at, cols_at, count, odd, center, *edges, probe, amps, high, low)
 
 
 def piece_kernel(index, sums, probe, out):
@@ -286,11 +289,25 @@
 SPLIT = {"y_lo": 4, "z_hi": 3, "z_lo": 4, "y_hi": 2, "x": 4, "core": 2}
 
 
-def neighbours(last, first, axis):
+def swaps(a, b, axis):
     peers = lax.axis_size(axis)
-    up = [(i, i + 1) for i in range(peers - 1)]
-    down = [(j, i) for i, j in up]
-    return lax.ppermute(last, axis, up), lax.ppermute(first, axis, down)
+
+    def swap(part, start):
+        pairs = [(i, i + 1) for i in range(start, peers - 1, 2)]
+        return lax.ppermute(part, axis, pairs + [(j, i) for i, j in pairs])
+
+    b = swap(b, 1)
+    return swap(a, 0), b
+
+
+def swapped(last, first, axis):
+    odd = lax.axis_index(axis) % 2 == 1
+    return swaps(jnp.where(odd, first, last), jnp.where(odd, last, first), axis)
+
+
+def in_order(a, b, axis):
+    odd = lax.axis_index(axis) % 2 == 1
+    return jnp.where(odd, a, b), jnp.where(odd, b, a)
 
 
 def exchanged(array, axes):
@@ -305,39 +322,39 @@
     rim = note.shape[0]
     th, tw = object_field.shape[1:]
     tail = jnp.broadcast_to(note, (2, TAIL, rim))
-    tail_wide = jnp.concatenate([tail] * (tw // rim), axis=2)
 
     def column(part):
-        return jnp.concatenate([tail, object_field[:, :, part], tail], axis=1)
+        return jnp.concatenate([object_field[:, :, part], tail], axis=1)
+
+    col_a, col_b = swapped(column(slice(tw - rim, tw)), column(slice(0, rim)), COL)
 
     def line(part):
-        return jnp.concatenate([object_field[:, part], tail_wide], axis=1)
-
-    def corner(part):
-        return jnp.concatenate([left[:, part], right[:, part]], axis=0)
-
-    left, right = neighbours(column(slice(tw - rim, tw)), column(slice(0, rim)), COL)
-    above, below = neighbours(line(slice(th - rim, th)), line(slice(0, rim)), ROW)
-    corners_above, corners_below = neighbours(
-        corner(slice(TAIL + th - rim, TAIL + th + TAIL)), corner(slice(0, TAIL + rim)), ROW
-    )
-    notes = [
-        corners_above[0, rim, :NOTE], above[0, rim, :NOTE], corners_above[2, rim, :NOTE],
-        left[0, 0, :NOTE], note[:NOTE], right[0, 0, :NOTE],
-        corners_below[0, 0, :NOTE], below[0, rim, :NOTE], corners_below[2, 0, :NOTE],
-    ]
-    edges = (above, below, left, right, corners_above, corners_below)
+        full = jnp.concatenate([col_a[:, part], object_field[:, part], col_b[:, part]], axis=2)
+        notes = jnp.concatenate([col_a[:, th:], tail, tail, col_b[:, th:]], axis=2)
+        return jnp.concatenate([full, notes], axis=1)
+
+    row_a, row_b = swapped(line(slice(th - rim, th)), line(slice(0, rim)), ROW)
+    left, right = in_order(col_a[0, th, :NOTE], col_b[0, th, :NOTE], COL)
+    above, below = in_order(row_a[0, rim], row_b[0, rim], ROW)
+
+    def three(row):
+        near, far = in_order(row[:NOTE], row[rim + tw : rim + tw + NOTE], COL)
+        return [near, row[rim : rim + NOTE], far]
+
+    notes = three(above) + [left, note[:NOTE], right] + three(below)
+    edges = (col_a, col_b, row_a, row_b)
     return edges, jnp.concatenate(notes).astype(jnp.int32)
 
 
-def folded(grad, above, below):
-    rim = above.shape[1]
+def folded(grad, a, b):
+    rim = a.shape[1]
     th = grad.shape[1]
-    from_above, from_below = neighbours(below, above, ROW)
+    from_above, from_below = in_order(*swaps(a, b, ROW), ROW)
     grad = jnp.concatenate(
         [grad[:, :rim] + from_above, grad[:, rim : th - rim], grad[:, th - rim :] + from_below], axis=1
     )
-    from_left, from_right = neighbours(grad[:, :, -rim:], grad[:, :, :rim], COL)
+    got = swapped(grad[:, :, -rim:], grad[:, :, :rim], COL)
+    from_left, from_right = in_order(*got, COL)
     grad = grad[:, :, rim:-rim]
     return jnp.concatenate([grad[:, :, :rim] + from_left, grad[:, :, rim:] + from_right], axis=2)
 
@@ -351,8 +368,9 @@
     own = jnp.concatenate([rows_at, cols_at, picks, scan_count])
     edges, scans_at = halo(object_field, jnp.pad(own.astype(F32), (0, rim - NOTE)))
     amps = ordered_amplitudes(amplitudes[0, 0], picks)
+    odd = jnp.stack([lax.axis_index(ROW), lax.axis_index(COL)]).astype(jnp.int32) % 2
     above, grad, below, sums = scans(
-        picks, rows_at, cols_at, scan_count, object_field, edges, probe_field, amps, near
+        picks, rows_at, cols_at, scan_count, odd, object_field, edges, probe_field, amps, near
     )
     share = light_share(scans_at, probe_field, th, tw)
     mine = exchanged(sums, NEAR).sum(0)

time: 186 us -> 162 us (0.87)
  the two profiles are of different devices: /device:TPU:15 before, /device:TPU:1 now
where the time goes in v3:
time: 162 us
  starting transfers between devices  58.5 us (36%)
  blocking collectives  57.1 us (35%)
  waiting for transfers between devices  20.1 us (12%)
  Pallas kernels  12 us (7%)
  other arithmetic  8.36 us (5%)
  local copies, waits for them, and re-layouts  3.81 us (2%)
  between operations  1.71 us (1%)
    all_to_all x4, blocking collectives, exchanged(): lax.all_to_all(array.reshape(lax.axis_size(axes), -1, array.shape[-1]), a...  57.1 us
    ppermute x8, starting transfers between devices, swap(): return lax.ppermute(part, axis, pairs + [(j, i) for i, j in pairs])  30.4 us
    all_to_all x2, starting transfers between devices, exchanged(): lax.all_to_all(array.reshape(lax.axis_size(axes), -1, array.shape[-1]), a...  28.2 us
    ppermute x8, waiting for transfers between devices, swap(): return lax.ppermute(part, axis, pairs + [(j, i) for i, j in pairs])  12.9 us
    all_to_all x2, waiting for transfers between devices, exchanged(): lax.all_to_all(array.reshape(lax.axis_size(axes), -1, array.shape[-1]), a...  7.12 us
    pallas_call x1, Pallas kernels, scans(): pl.pallas_call(scan_kernel, in_specs=[smem] * 5 + [vmem] * 9, out_specs=[...  5.56 us
    pallas_call x1, Pallas kernels, light_share(): pl.pallas_call(light_kernel, in_specs=[pl.BlockSpec(memory_space=pltpu.SM...  3.53 us
  transfers between devices with their start and end apart: 10, of which 3 were waited for; matrix products, arithmetic and copies ran while one was open for 4% of the time, Pallas kernels for 3%

profile of v3, /device:TPU:1, one launch (start us, length us, event | category | flops | bytes accessed | tf_op | source)
XLA Modules:
  0.0 161.6 jit_solution(9660211248432173721)
XLA Ops:
  1.3 1.2 fusion.13
  2.6 0.1 add_convert_fusion
  2.7 0.1 fusion.3
  2.8 4.5 %collective-permute-start.1 = (f32[2,392,128]{2,1,0:T(8,128)S(1)}, f32[2,392,128]{2,1,0:T(8,128)S(1)}, u32[]{:S(2)}, u32[]{:S(2)}) collective-permute-start(f32[2,392,128]{2,1,0:T(8,128)S(1)} %get-tuple-element.31), channel_id=1, source_target_pairs={{1,2},{3,4},{5,6},{7,8},{9,10},{11,12},{13,14},{2,1},{4,3},{6,5},{... | collective-permute-start | bytes 1204232 | tf_op jit(solution)/shard_map/ppermute | solution.py:297
  7.3 8.6 %collective-permute-start = (f32[2,392,128]{2,1,0:T(8,128)S(1)}, f32[2,392,128]{2,1,0:T(8,128)S(1)}, u32[]{:S(2)}, u32[]{:S(2)}) collective-permute-start(f32[2,392,128]{2,1,0:T(8,128)S(1)} %get-tuple-element.32), channel_id=1, source_target_pairs={{0,1},{2,3},{4,5},{6,7},{8,9},{10,11},{12,13},{14,15},{1,0},{3,2},... | collective-permute-start | bytes 1204232 | tf_op jit(solution)/shard_map/ppermute | solution.py:297
  15.9 0.0 collective-permute-done.1.col_b
  16.0 1.2 collective-permute-done.col_a
  17.2 0.7 copy-done.2
  17.9 0.1 broadcast_select_fusion
  18.0 0.0 copy-start.1
  18.0 0.0 copy-start.6
  18.1 0.0 copy-start.7
  18.1 0.1 broadcast_select_fusion.1
  18.1 2.1 %collective-permute-start.2 = (f32[2,136,512]{2,1,0:T(8,128)S(1)}, f32[2,136,512]{2,1,0:T(8,128)S(1)}, u32[]{:S(2)}, u32[]{:S(2)}) collective-permute-start(f32[2,136,512]{2,1,0:T(8,128)S(1)} %broadcast_select_fusion.1), channel_id=1, source_target_pairs={{0,16},{32,48},{64,80},{96,112},{128,144},{160,176},{192,208},{224... | collective-permute-start | bytes 1671176 | tf_op jit(solution)/shard_map/ppermute | solution.py:297
  20.2 0.7 collective-permute-start.3
  20.9 1.2 amplitude_order.1.amps
  22.2 0.1 and_select_fusion.odd
  22.3 11.7 %collective-permute-done.2.row_a = f32[2,136,512]{2,1,0:T(8,128)S(1)} collective-permute-done((f32[2,136,512]{2,1,0:T(8,128)S(1)}, f32[2,136,512]{2,1,0:T(8,128)S(1)}, u32[]{:S(2)}, u32[]{:S(2)}) %collective-permute-start.2) | collective-permute-done | bytes 557088 | tf_op jit(solution)/shard_map/ppermute | solution.py:297
  34.0 0.0 collective-permute-done.3.row_b
  34.0 0.0 copy-start.5
  34.0 5.6 %scan_step.1 = (f32[2,128,512]{2,1,0:T(8,128)S(1)}, f32[2,384,512]{2,1,0:T(8,128)S(1)}, f32[2,128,512]{2,1,0:T(8,128)S(1)}, f32[8,192,128]{2,1,0:T(8,128)S(1)}) custom-call(s32[2]{0:T(128)S(1)} %bitcast.29, s32[4]{0:T(128)S(1)} %bitcast.31, s32[4]{0:T(128)S(1)} %bitcast.33, s32[1]{0:T(128)S(6)} %copy.11.count, s32[2]{0:T(128)S(1)} %and_select_fusion.odd, ...), custom_call_target="tpu_custom_call" | custom-call | tf_op jit(solution)/shard_map/scan_step/pallas_call | solution.py:182
  39.6 0.8 copy-done.13
  40.4 0.8 copy-done.14
  41.2 16.4 %all_to_all.30 = f32[8,192,128]{2,1,0:T(8,128)} all-to-all(f32[8,192,128]{2,1,0:T(8,128)S(1)} %get-tuple-element.14), channel_id=1, replica_groups=mesh['y_lo'=4,'z_hi'=3,'z_lo'=4,'y_hi'=2,'x'=4,'core'=2] {'x','core'}, dimensions={0} | all-to-all | bytes 1572864 | tf_op jit(solution)/shard_map/all_to_all | solution.py:314
  57.7 1.8 %reduce_sum.36 = f32[192,128]{1,0:T(8,128)} reduce(f32[8,192,128]{2,1,0:T(8,128)} %all_to_all.30, f32[]{:T(128)} %constant.75.clone.1), dimensions={0}, to_apply=%region_0.1 | reduce | flops 172032 | bytes 884740 | tf_op jit(solution)/shard_map/reduce_sum | solution.py:376
  59.5 7.4 %collective-permute-start.4 = (f32[2,128,512]{2,1,0:T(8,128)}, f32[2,128,512]{2,1,0:T(8,128)}, u32[]{:S(2)}, u32[]{:S(2)}) collective-permute-start(f32[2,128,512]{2,1,0:T(8,128)} %copy-done.14), channel_id=1, source_target_pairs={{0,16},{32,48},{64,80},{96,112},{128,144},{160,176},{192,208},{224... | collective-permute-start | bytes 1572872 | tf_op jit(solution)/shard_map/ppermute | solution.py:297
  66.9 1.5 collective-permute-start.5
  68.4 0.7 fusion.8
  69.1 0.7 broadcast_select_fusion.2
  69.8 20.6 %all-to-all-start.1 = ((f32[8,24,128]{2,1,0:T(8,128)}), f32[8,24,128]{2,1,0:T(8,128)S(1)}, u32[]{:S(2)}, u32[]{:S(2)}) async-start(f32[8,24,128]{2,1,0:T(8,128)} %bitcast.14), calls=%async_computation.1 | async-start | bytes 196608 | tf_op jit(solution)/shard_map/all_to_all | solution.py:314
  90.5 0.0 collective-permute-done.4
  90.5 1.4 select_add_fusion.1
  91.9 0.1 pad_maximum_fusion
  92.1 0.9 slice_select_fusion.1
  93.0 3.5 %collective-permute-start.6 = (f32[2,384,128]{2,1,0:T(8,128)}, f32[2,384,128]{2,1,0:T(8,128)}, u32[]{:S(2)}, u32[]{:S(2)}) collective-permute-start(f32[2,384,128]{2,1,0:T(8,128)} %get-tuple-element.24), channel_id=1, source_target_pairs={{0,1},{2,3},{4,5},{6,7},{8,9},{10,11},{12,13},{14,15},{1,0},{3,2},... | collective-permute-start | bytes 1179656 | tf_op jit(solution)/shard_map/ppermute | solution.py:297
  96.5 2.1 %collective-permute-start.7 = (f32[2,384,128]{2,1,0:T(8,128)}, f32[2,384,128]{2,1,0:T(8,128)}, u32[]{:S(2)}, u32[]{:S(2)}) collective-permute-start(f32[2,384,128]{2,1,0:T(8,128)} %get-tuple-element.25), channel_id=1, source_target_pairs={{1,2},{3,4},{5,6},{7,8},{9,10},{11,12},{13,14},{2,1},{4,3},{6,5},{... | collective-permute-start | bytes 1179656 | tf_op jit(solution)/shard_map/ppermute | solution.py:297
  98.7 0.1 concatenate.44
  98.7 3.5 %light_share.1 = f32[384,256]{1,0:T(8,128)S(1)} custom-call(s32[99]{0:T(128)S(1)} %convert_element_type.21.scans_at, f32[2,256,256]{2,1,0:T(8,128)S(1)} %copy-done.1), custom_call_target="tpu_custom_call" | custom-call | flops 20000000 | bytes 1000000 | tf_op jit(solution)/shard_map/light_share/pallas_call | solution.py:273
  102.3 6.9 %all_to_all.31 = f32[4,24,128]{2,1,0:T(8,128)S(1)} all-to-all(f32[4,24,128]{2,1,0:T(8,128)S(1)} %broadcast_in_dim.9), channel_id=1, replica_groups=mesh['y_lo'=4,'z_hi'=3,'z_lo'=4,'y_hi'=2,'x'=4,'core'=2] {'z_lo'}, dimensions={0} | all-to-all | bytes 98304 | tf_op jit(solution)/shard_map/all_to_all | solution.py:314
  109.3 16.1 %all_to_all.32 = f32[3,24,128]{2,1,0:T(8,128)S(1)} all-to-all(f32[3,24,128]{2,1,0:T(8,128)S(1)} %broadcast_in_dim.10), channel_id=1, replica_groups=mesh['y_lo'=4,'z_hi'=3,'z_lo'=4,'y_hi'=2,'x'=4,'core'=2] {'z_hi'}, dimensions={0} | all-to-all | bytes 73728 | tf_op jit(solution)/shard_map/all_to_all | solution.py:314
  125.4 17.6 %all_to_all.33 = f32[8,24,128]{2,1,0:T(8,128)S(1)} all-to-all(f32[8,24,128]{2,1,0:T(8,128)S(1)} %broadcast_in_dim.11), channel_id=1, replica_groups=mesh['y_lo'=4,'z_hi'=3,'z_lo'=4,'y_hi'=2,'x'=4,'core'=2] {'y_lo','y_hi'}, dimensions={0} | all-to-all | bytes 196608 | tf_op jit(solution)/shard_map/all_to_all | solution.py:314
  143.0 0.9 probe_piece.1
  143.8 7.5 %all-to-all-start.5 = ((f32[8,128,128]{2,1,0:T(8,128)}), f32[8,128,128]{2,1,0:T(8,128)S(1)}, u32[]{:S(2)}, u32[]{:S(2)}) async-start(f32[8,128,128]{2,1,0:T(8,128)} %probe_piece.1), calls=%async_computation.5 | async-start | bytes 1048576 | tf_op jit(solution)/shard_map/all_to_all | solution.py:314
  151.4 0.0 collective-permute-done.7
  151.4 1.2 slice_add_fusion.1
  152.6 1.0 fusion
  153.6 7.1 %all-to-all-done.5.pieces = f32[8,128,128]{2,1,0:T(8,128)S(1)} async-done(((f32[8,128,128]{2,1,0:T(8,128)}), f32[8,128,128]{2,1,0:T(8,128)S(1)}, u32[]{:S(2)}, u32[]{:S(2)}) %all-to-all-start.5) | async-done | bytes 524320 | tf_op jit(solution)/shard_map/all_to_all | solution.py:314
  160.7 0.8 probe_join.1
  (41 shorter events, 0.2 us)
Async XLA Ops:
  0.6 2.0 %copy-start.10 = (s32[1,1,2]{2,1,0:T(1,128)S(1)}, s32[1,1,2]{2,1,0:T(1,128)}, u32[]{:S(2)}) copy-start(s32[1,1,2]{2,1,0:T(1,128)} %param.14) | copy-start | bytes 28
  0.6 2.0 %copy-start.12 = (s32[1,1,4]{2,1,0:T(1,128)S(1)}, s32[1,1,4]{2,1,0:T(1,128)}, u32[]{:S(2)}) copy-start(s32[1,1,4]{2,1,0:T(1,128)} %param.13) | copy-start | bytes 52
  0.7 2.0 %copy-start.11 = (s32[1,1,4]{2,1,0:T(1,128)S(1)}, s32[1,1,4]{2,1,0:T(1,128)}, u32[]{:S(2)}) copy-start(s32[1,1,4]{2,1,0:T(1,128)} %param.12) | copy-start | bytes 52
  1.3 14.6 %copy-start = (f32[2,384,256]{2,1,0:T(8,128)S(1)}, f32[2,384,256]{2,1,0:T(8,128)}, u32[]{:S(2)}) copy-start(f32[2,384,256]{2,1,0:T(8,128)} %center.1) | copy-start | bytes 2359300
  2.8 13.2 %collective-permute-start.1 = (f32[2,392,128]{2,1,0:T(8,128)S(1)}, f32[2,392,128]{2,1,0:T(8,128)S(1)}, u32[]{:S(2)}, u32[]{:S(2)}) collective-permute-start(f32[2,392,128]{2,1,0:T(8,128)S(1)} %get-tuple-element.31), channel_id=1, source_target_pairs={{1,2},{3,4},{5,6},{7,8},{9,10},{11,12},{13,14},{2,1},{4,3},{6,5},{... | collective-permute-start | bytes 1204232 | tf_op jit(solution)/shard_map/ppermute | solution.py:297
  7.3 9.9 %collective-permute-start = (f32[2,392,128]{2,1,0:T(8,128)S(1)}, f32[2,392,128]{2,1,0:T(8,128)S(1)}, u32[]{:S(2)}, u32[]{:S(2)}) collective-permute-start(f32[2,392,128]{2,1,0:T(8,128)S(1)} %get-tuple-element.32), channel_id=1, source_target_pairs={{0,1},{2,3},{4,5},{6,7},{8,9},{10,11},{12,13},{14,15},{1,0},{3,2},... | collective-permute-start | bytes 1204232 | tf_op jit(solution)/shard_map/ppermute | solution.py:297
  17.2 0.7 copy-start.2
  17.9 3.0 %copy-start.8 = (bf16[1,1,4,256,256]{4,3,2,1,0:T(8,128)(2,1)S(1)}, bf16[1,1,4,256,256]{4,3,2,1,0:T(8,128)(2,1)}, u32[]{:S(2)}) copy-start(bf16[1,1,4,256,256]{4,3,2,1,0:T(8,128)(2,1)} %param.11) | copy-start | bytes 1572868
  17.9 3.0 %copy-start.9 = (bf16[256,256]{1,0:T(8,128)(2,1)S(1)}, bf16[256,256]{1,0:T(8,128)(2,1)}, u32[]{:S(2)}) copy-start(bf16[256,256]{1,0:T(8,128)(2,1)} %constant.76.clone.order) | copy-start | bytes 393220
  18.0 16.0 %copy-start.1 = (f32[2,256,256]{2,1,0:T(8,128)S(1)}, f32[2,256,256]{2,1,0:T(8,128)}, u32[]{:S(2)}) copy-start(f32[2,256,256]{2,1,0:T(8,128)} %probe.5) | copy-start | bytes 1572868
  18.0 16.0 %copy-start.3 = (f32[2,392,128]{2,1,0:T(8,128)S(1)}, f32[2,392,128]{2,1,0:T(8,128)}, u32[]{:S(2)}) copy-start(f32[2,392,128]{2,1,0:T(8,128)} %copy-done.2) | copy-start | bytes 1204228
  18.0 16.0 %copy-start.6 = (bf16[4,256,256]{2,1,0:T(8,128)(2,1)S(1)}, bf16[4,256,256]{2,1,0:T(8,128)(2,1)}, u32[]{:S(2)}) copy-start(bf16[4,256,256]{2,1,0:T(8,128)(2,1)} %constant.88.low) | copy-start | bytes 1572868
  18.1 16.0 %copy-start.7 = (bf16[4,256,256]{2,1,0:T(8,128)(2,1)S(1)}, bf16[4,256,256]{2,1,0:T(8,128)(2,1)}, u32[]{:S(2)}) copy-start(bf16[4,256,256]{2,1,0:T(8,128)(2,1)} %constant.85.high) | copy-start | bytes 1572868
  18.1 15.8 %collective-permute-start.2 = (f32[2,136,512]{2,1,0:T(8,128)S(1)}, f32[2,136,512]{2,1,0:T(8,128)S(1)}, u32[]{:S(2)}, u32[]{:S(2)}) collective-permute-start(f32[2,136,512]{2,1,0:T(8,128)S(1)} %broadcast_select_fusion.1), channel_id=1, source_target_pairs={{0,16},{32,48},{64,80},{96,112},{128,144},{160,176},{192,208},{224... | collective-permute-start | bytes 1671176 | tf_op jit(solution)/shard_map/ppermute | solution.py:297
  20.2 13.8 %collective-permute-start.3 = (f32[2,136,512]{2,1,0:T(8,128)S(1)}, f32[2,136,512]{2,1,0:T(8,128)S(1)}, u32[]{:S(2)}, u32[]{:S(2)}) collective-permute-start(f32[2,136,512]{2,1,0:T(8,128)S(1)} %broadcast_select_fusion), channel_id=1, source_target_pairs={{16,32},{48,64},{80,96},{112,128},{144,160},{176,192},{208,224},{2... | collective-permute-start | bytes 1671176 | tf_op jit(solution)/shard_map/ppermute | solution.py:297
  34.0 5.6 %copy-start.4 = (f32[2,136,512]{2,1,0:T(8,128)}, f32[2,136,512]{2,1,0:T(8,128)S(1)}, u32[]{:S(2)}) copy-start(f32[2,136,512]{2,1,0:T(8,128)S(1)} %collective-permute-done.2.row_a) | copy-start | bytes 1671172
  34.0 5.6 %copy-start.5 = (f32[2,136,512]{2,1,0:T(8,128)}, f32[2,136,512]{2,1,0:T(8,128)S(1)}, u32[]{:S(2)}) copy-start(f32[2,136,512]{2,1,0:T(8,128)S(1)} %collective-permute-done.3.row_b) | copy-start | bytes 1671172
  39.6 0.8 copy-start.13
  40.4 0.8 copy-start.14
  59.5 31.0 %collective-permute-start.4 = (f32[2,128,512]{2,1,0:T(8,128)}, f32[2,128,512]{2,1,0:T(8,128)}, u32[]{:S(2)}, u32[]{:S(2)}) collective-permute-start(f32[2,128,512]{2,1,0:T(8,128)} %copy-done.14), channel_id=1, source_target_pairs={{0,16},{32,48},{64,80},{96,112},{128,144},{160,176},{192,208},{224... | collective-permute-start | bytes 1572872 | tf_op jit(solution)/shard_map/ppermute | solution.py:297
  66.9 23.6 %collective-permute-start.5 = (f32[2,128,512]{2,1,0:T(8,128)}, f32[2,128,512]{2,1,0:T(8,128)}, u32[]{:S(2)}, u32[]{:S(2)}) collective-permute-start(f32[2,128,512]{2,1,0:T(8,128)} %copy-done.13), channel_id=1, source_target_pairs={{16,32},{48,64},{80,96},{112,128},{144,160},{176,192},{208,224},{2... | collective-permute-start | bytes 1572872 | tf_op jit(solution)/shard_map/ppermute | solution.py:297
  69.8 32.5 %all-to-all-start.1 = ((f32[8,24,128]{2,1,0:T(8,128)}), f32[8,24,128]{2,1,0:T(8,128)S(1)}, u32[]{:S(2)}, u32[]{:S(2)}) async-start(f32[8,24,128]{2,1,0:T(8,128)} %bitcast.14), calls=%async_computation.1 | async-start | bytes 196608 | tf_op jit(solution)/shard_map/all_to_all | solution.py:314
  93.0 58.4 %collective-permute-start.6 = (f32[2,384,128]{2,1,0:T(8,128)}, f32[2,384,128]{2,1,0:T(8,128)}, u32[]{:S(2)}, u32[]{:S(2)}) collective-permute-start(f32[2,384,128]{2,1,0:T(8,128)} %get-tuple-element.24), channel_id=1, source_target_pairs={{0,1},{2,3},{4,5},{6,7},{8,9},{10,11},{12,13},{14,15},{1,0},{3,2},... | collective-permute-start | bytes 1179656 | tf_op jit(solution)/shard_map/ppermute | solution.py:297
  96.5 54.9 %collective-permute-start.7 = (f32[2,384,128]{2,1,0:T(8,128)}, f32[2,384,128]{2,1,0:T(8,128)}, u32[]{:S(2)}, u32[]{:S(2)}) collective-permute-start(f32[2,384,128]{2,1,0:T(8,128)} %get-tuple-element.25), channel_id=1, source_target_pairs={{1,2},{3,4},{5,6},{7,8},{9,10},{11,12},{13,14},{2,1},{4,3},{6,5},{... | collective-permute-start | bytes 1179656 | tf_op jit(solution)/shard_map/ppermute | solution.py:297
  143.8 16.9 %all-to-all-start.5 = ((f32[8,128,128]{2,1,0:T(8,128)}), f32[8,128,128]{2,1,0:T(8,128)S(1)}, u32[]{:S(2)}, u32[]{:S(2)}) async-start(f32[8,128,128]{2,1,0:T(8,128)} %probe_piece.1), calls=%async_computation.5 | async-start | bytes 1048576 | tf_op jit(solution)/shard_map/all_to_all | solution.py:314

commit v4 on v3

--- a/solution.py
+++ b/solution.py
@@ -346,13 +346,16 @@
     return edges, jnp.concatenate(notes).astype(jnp.int32)
 
 
-def folded(grad, a, b):
+def row_folded(grad, a, b):
     rim = a.shape[1]
     th = grad.shape[1]
     from_above, from_below = in_order(*swaps(a, b, ROW), ROW)
-    grad = jnp.concatenate(
+    return jnp.concatenate(
         [grad[:, :rim] + from_above, grad[:, rim : th - rim], grad[:, th - rim :] + from_below], axis=1
     )
+
+
+def col_folded(grad, rim):
     got = swapped(grad[:, :, -rim:], grad[:, :, :rim], COL)
     from_left, from_right = in_order(*got, COL)
     grad = grad[:, :, rim:-rim]
@@ -373,12 +376,14 @@
         picks, rows_at, cols_at, scan_count, odd, object_field, edges, probe_field, amps, near
     )
     share = light_share(scans_at, probe_field, th, tw)
-    mine = exchanged(sums, NEAR).sum(0)
-    above, below, mine = lax.optimization_barrier((above, below, mine))
+    mine = exchanged(sums, NEAR)
+    share, mine = lax.optimization_barrier((share, mine))
+    mine = mine.sum(0)
+    grad = row_folded(grad, above, below)
     mine = exchanged(mine, MID)
-    share, mine = lax.optimization_barrier((share, mine))
-    grad = folded(grad, above, below)
+    grad, mine = lax.optimization_barrier((grad, mine))
     mine = mine.sum(0)
+    grad = col_folded(grad, rim)
     mine = exchanged(copied(mine, ("z_lo",)), ("z_lo",)).sum(0)
     mine = exchanged(copied(mine, ("z_hi",)), ("z_hi",)).sum(0)
     mine = exchanged(copied(mine, MID), MID).reshape(-1, rim)

time: 162 us -> 152 us (0.938)
  blocking collectives: 57.1 us -> 26.2 us
  starting transfers between devices: 58.5 us -> 72.9 us
  waiting for transfers between devices: 20.1 us -> 25.2 us
    all_to_all x4 -> x3, blocking collectives: 57.1 us -> 26.2 us  [exchanged(): lax.all_to_all(array.reshape(lax.axis_size(axes), -1, array.shape[-1]), a...]
    all_to_all x2 -> x3, starting transfers between devices: 28.2 us -> 42 us  [exchanged(): lax.all_to_all(array.reshape(lax.axis_size(axes), -1, array.shape[-1]), a...]
    all_to_all x2 -> x3, waiting for transfers between devices: 7.12 us -> 12.3 us  [exchanged(): lax.all_to_all(array.reshape(lax.axis_size(axes), -1, array.shape[-1]), a...]
    reduce_sum x1 -> x0, other arithmetic: 1.83 us -> none  [per_device(): mine = exchanged(sums, NEAR).sum(0)]
    reduce_sum x1 -> x2, other arithmetic: 0.01 us -> 1.84 us  [per_device(): mine = mine.sum(0)]
    unnamed x30 -> x32, local copies, waits for them, and re-layouts: 2.38 us -> 3.26 us
  transfers between devices with their start and end apart: 10 -> 11, of which waited for: 3 -> 4; matrix products, arithmetic and copies ran while one was open for 4% -> 5% of each run, Pallas kernels for 3% -> 4%
where the time goes in v4:
time: 152 us; the launch traced here: 151 us
  starting transfers between devices  72.9 us (48%)
  blocking collectives  26.2 us (17%)
  waiting for transfers between devices  25.2 us (17%)
  Pallas kernels  11.8 us (8%)
  other arithmetic  8.36 us (6%)
  local copies, waits for them, and re-layouts  4.7 us (3%)
  between operations  1.7 us (1%)
    all_to_all x3, starting transfers between devices, exchanged(): lax.all_to_all(array.reshape(lax.axis_size(axes), -1, array.shape[-1]), a...  42 us
    ppermute x8, starting transfers between devices, swap(): return lax.ppermute(part, axis, pairs + [(j, i) for i, j in pairs])  30.9 us
    all_to_all x3, blocking collectives, exchanged(): lax.all_to_all(array.reshape(lax.axis_size(axes), -1, array.shape[-1]), a...  26.2 us
    ppermute x8, waiting for transfers between devices, swap(): return lax.ppermute(part, axis, pairs + [(j, i) for i, j in pairs])  12.9 us
    all_to_all x3, waiting for transfers between devices, exchanged(): lax.all_to_all(array.reshape(lax.axis_size(axes), -1, array.shape[-1]), a...  12.3 us
    pallas_call x1, Pallas kernels, scans(): pl.pallas_call(scan_kernel, in_specs=[smem] * 5 + [vmem] * 9, out_specs=[...  5.47 us
    pallas_call x1, Pallas kernels, light_share(): pl.pallas_call(light_kernel, in_specs=[pl.BlockSpec(memory_space=pltpu.SM...  3.42 us
    unnamed x32, local copies, waits for them, and re-layouts  3.26 us
  transfers between devices with their start and end apart: 11, of which 4 were waited for; matrix products, arithmetic and copies ran while one was open for 5% of the time, Pallas kernels for 4%

profile of v4, /device:TPU:1, one launch (start us, length us, event | category | flops | bytes accessed | tf_op | source)
XLA Modules:
  0.0 150.9 jit_solution(4183308374881481186)
XLA Ops:
  1.3 1.2 fusion.13
  2.6 0.1 add_convert_fusion
  2.7 0.1 fusion.3
  2.8 4.5 %collective-permute-start.1 = (f32[2,392,128]{2,1,0:T(8,128)S(1)}, f32[2,392,128]{2,1,0:T(8,128)S(1)}, u32[]{:S(2)}, u32[]{:S(2)}) collective-permute-start(f32[2,392,128]{2,1,0:T(8,128)S(1)} %get-tuple-element.29), channel_id=1, source_target_pairs={{1,2},{3,4},{5,6},{7,8},{9,10},{11,12},{13,14},{2,1},{4,3},{6,5},{... | collective-permute-start | bytes 1204232 | tf_op jit(solution)/shard_map/ppermute | solution.py:297
  7.3 8.6 %collective-permute-start = (f32[2,392,128]{2,1,0:T(8,128)S(1)}, f32[2,392,128]{2,1,0:T(8,128)S(1)}, u32[]{:S(2)}, u32[]{:S(2)}) collective-permute-start(f32[2,392,128]{2,1,0:T(8,128)S(1)} %get-tuple-element.30), channel_id=1, source_target_pairs={{0,1},{2,3},{4,5},{6,7},{8,9},{10,11},{12,13},{14,15},{1,0},{3,2},... | collective-permute-start | bytes 1204232 | tf_op jit(solution)/shard_map/ppermute | solution.py:297
  16.0 1.2 collective-permute-done.col_a
  17.2 0.7 copy-done.2
  18.0 0.1 broadcast_select_fusion
  18.0 0.0 copy-start.1
  18.0 0.0 copy-start.7
  18.1 0.0 copy-start.8
  18.1 0.1 broadcast_select_fusion.1
  18.1 2.1 %collective-permute-start.2 = (f32[2,136,512]{2,1,0:T(8,128)S(1)}, f32[2,136,512]{2,1,0:T(8,128)S(1)}, u32[]{:S(2)}, u32[]{:S(2)}) collective-permute-start(f32[2,136,512]{2,1,0:T(8,128)S(1)} %broadcast_select_fusion.1), channel_id=1, source_target_pairs={{0,16},{32,48},{64,80},{96,112},{128,144},{160,176},{192,208},{224... | collective-permute-start | bytes 1671176 | tf_op jit(solution)/shard_map/ppermute | solution.py:297
  20.2 0.7 collective-permute-start.3
  20.9 1.2 amplitude_order.1.amps
  22.2 0.1 and_select_fusion.odd
  22.3 11.7 %collective-permute-done.2.row_a = f32[2,136,512]{2,1,0:T(8,128)S(1)} collective-permute-done((f32[2,136,512]{2,1,0:T(8,128)S(1)}, f32[2,136,512]{2,1,0:T(8,128)S(1)}, u32[]{:S(2)}, u32[]{:S(2)}) %collective-permute-start.2) | collective-permute-done | bytes 557088 | tf_op jit(solution)/shard_map/ppermute | solution.py:297
  34.0 0.0 collective-permute-done.3.row_b
  34.0 5.5 %scan_step.1 = (f32[2,128,512]{2,1,0:T(8,128)S(1)}, f32[2,384,512]{2,1,0:T(8,128)S(1)}, f32[2,128,512]{2,1,0:T(8,128)S(1)}, f32[8,192,128]{2,1,0:T(8,128)S(1)}) custom-call(s32[2]{0:T(128)S(1)} %bitcast.29, s32[4]{0:T(128)S(1)} %bitcast.31, s32[4]{0:T(128)S(1)} %bitcast.33, s32[1]{0:T(128)S(6)} %copy.11.count, s32[2]{0:T(128)S(1)} %and_select_fusion.odd, ...), custom_call_target="tpu_custom_call" | custom-call | tf_op jit(solution)/shard_map/scan_step/pallas_call | solution.py:182
  39.5 0.0 copy-start.4
  39.5 0.9 copy-done.4
  40.4 0.8 copy-done.14
  41.2 0.8 copy-done.15
  42.0 5.3 %all-to-all-start = ((f32[8,192,128]{2,1,0:T(8,128)}), f32[8,192,128]{2,1,0:T(8,128)}, u32[]{:S(2)}, u32[]{:S(2)}) async-start(f32[8,192,128]{2,1,0:T(8,128)} %copy-done.4), calls=%async_computation | async-start | bytes 1572864 | tf_op jit(solution)/shard_map/all_to_all | solution.py:314
  47.3 6.5 %collective-permute-start.4 = (f32[2,128,512]{2,1,0:T(8,128)}, f32[2,128,512]{2,1,0:T(8,128)}, u32[]{:S(2)}, u32[]{:S(2)}) collective-permute-start(f32[2,128,512]{2,1,0:T(8,128)} %copy-done.15), channel_id=1, source_target_pairs={{0,16},{32,48},{64,80},{96,112},{128,144},{160,176},{192,208},{224... | collective-permute-start | bytes 1572872 | tf_op jit(solution)/shard_map/ppermute | solution.py:297
  53.9 1.5 collective-permute-start.5
  55.3 0.7 fusion.8
  56.0 0.7 broadcast_select_fusion.2
  56.8 0.1 concatenate.43
  56.9 3.4 %light_share.1 = f32[384,256]{1,0:T(8,128)S(1)} custom-call(s32[99]{0:T(128)S(1)} %convert_element_type.21.scans_at, f32[2,256,256]{2,1,0:T(8,128)S(1)} %copy-done.1), custom_call_target="tpu_custom_call" | custom-call | flops 20000000 | bytes 1000000 | tf_op jit(solution)/shard_map/light_share/pallas_call | solution.py:273
  60.3 1.8 %reduce_sum.36 = f32[192,128]{1,0:T(8,128)} reduce(f32[8,192,128]{2,1,0:T(8,128)} %all-to-all-done, f32[]{:T(128)} %constant.75.clone.1), dimensions={0}, to_apply=%region_0.1 | reduce | flops 172032 | bytes 884740 | tf_op jit(solution)/shard_map/reduce_sum | solution.py:381
  62.1 23.8 %all-to-all-start.1 = ((f32[8,24,128]{2,1,0:T(8,128)}), f32[8,24,128]{2,1,0:T(8,128)S(1)}, u32[]{:S(2)}, u32[]{:S(2)}) async-start(f32[8,24,128]{2,1,0:T(8,128)} %bitcast.14), calls=%async_computation.1 | async-start | bytes 196608 | tf_op jit(solution)/shard_map/all_to_all | solution.py:314
  86.0 0.0 collective-permute-done.4
  86.0 1.5 select_add_fusion.1
  87.5 0.1 pad_maximum_fusion
  87.6 5.1 %all-to-all-done.1 = f32[8,24,128]{2,1,0:T(8,128)S(1)} async-done(((f32[8,24,128]{2,1,0:T(8,128)}), f32[8,24,128]{2,1,0:T(8,128)S(1)}, u32[]{:S(2)}, u32[]{:S(2)}) %all-to-all-start.1) | async-done | bytes 98336 | tf_op jit(solution)/shard_map/all_to_all | solution.py:314
  92.7 0.9 slice_select_fusion.1
  93.7 3.5 %collective-permute-start.6 = (f32[2,384,128]{2,1,0:T(8,128)}, f32[2,384,128]{2,1,0:T(8,128)}, u32[]{:S(2)}, u32[]{:S(2)}) collective-permute-start(f32[2,384,128]{2,1,0:T(8,128)} %get-tuple-element.22), channel_id=1, source_target_pairs={{0,1},{2,3},{4,5},{6,7},{8,9},{10,11},{12,13},{14,15},{1,0},{3,2},... | collective-permute-start | bytes 1179656 | tf_op jit(solution)/shard_map/ppermute | solution.py:297
  97.1 3.6 %collective-permute-start.7 = (f32[2,384,128]{2,1,0:T(8,128)}, f32[2,384,128]{2,1,0:T(8,128)}, u32[]{:S(2)}, u32[]{:S(2)}) collective-permute-start(f32[2,384,128]{2,1,0:T(8,128)} %get-tuple-element.23), channel_id=1, source_target_pairs={{1,2},{3,4},{5,6},{7,8},{9,10},{11,12},{13,14},{2,1},{4,3},{6,5},{... | collective-permute-start | bytes 1179656 | tf_op jit(solution)/shard_map/ppermute | solution.py:297
  100.8 6.9 %all_to_all.30 = f32[4,24,128]{2,1,0:T(8,128)S(1)} all-to-all(f32[4,24,128]{2,1,0:T(8,128)S(1)} %broadcast_in_dim.9), channel_id=1, replica_groups=mesh['y_lo'=4,'z_hi'=3,'z_lo'=4,'y_hi'=2,'x'=4,'core'=2] {'z_lo'}, dimensions={0} | all-to-all | bytes 98304 | tf_op jit(solution)/shard_map/all_to_all | solution.py:314
  107.7 10.2 %all_to_all.31 = f32[3,24,128]{2,1,0:T(8,128)S(1)} all-to-all(f32[3,24,128]{2,1,0:T(8,128)S(1)} %broadcast_in_dim.10), channel_id=1, replica_groups=mesh['y_lo'=4,'z_hi'=3,'z_lo'=4,'y_hi'=2,'x'=4,'core'=2] {'z_hi'}, dimensions={0} | all-to-all | bytes 73728 | tf_op jit(solution)/shard_map/all_to_all | solution.py:314
  118.0 9.1 %all_to_all.32 = f32[8,24,128]{2,1,0:T(8,128)S(1)} all-to-all(f32[8,24,128]{2,1,0:T(8,128)S(1)} %broadcast_in_dim.11), channel_id=1, replica_groups=mesh['y_lo'=4,'z_hi'=3,'z_lo'=4,'y_hi'=2,'x'=4,'core'=2] {'y_lo','y_hi'}, dimensions={0} | all-to-all | bytes 196608 | tf_op jit(solution)/shard_map/all_to_all | solution.py:314
  127.1 0.9 probe_piece.1
  127.9 12.8 %all-to-all-start.5 = ((f32[8,128,128]{2,1,0:T(8,128)}), f32[8,128,128]{2,1,0:T(8,128)S(1)}, u32[]{:S(2)}, u32[]{:S(2)}) async-start(f32[8,128,128]{2,1,0:T(8,128)} %probe_piece.1), calls=%async_computation.5 | async-start | bytes 1048576 | tf_op jit(solution)/shard_map/all_to_all | solution.py:314
  140.7 1.2 select_add_fusion.3
  141.9 1.0 fusion
  142.9 7.2 %all-to-all-done.5.pieces = f32[8,128,128]{2,1,0:T(8,128)S(1)} async-done(((f32[8,128,128]{2,1,0:T(8,128)}), f32[8,128,128]{2,1,0:T(8,128)S(1)}, u32[]{:S(2)}, u32[]{:S(2)}) %all-to-all-start.5) | async-done | bytes 524320 | tf_op jit(solution)/shard_map/all_to_all | solution.py:314
  150.1 0.8 probe_join.1
  (44 shorter events, 0.2 us)
Async XLA Ops:
  0.6 2.0 %copy-start.11 = (s32[1,1,2]{2,1,0:T(1,128)S(1)}, s32[1,1,2]{2,1,0:T(1,128)}, u32[]{:S(2)}) copy-start(s32[1,1,2]{2,1,0:T(1,128)} %param.14) | copy-start | bytes 28
  0.6 2.0 %copy-start.13 = (s32[1,1,4]{2,1,0:T(1,128)S(1)}, s32[1,1,4]{2,1,0:T(1,128)}, u32[]{:S(2)}) copy-start(s32[1,1,4]{2,1,0:T(1,128)} %param.13) | copy-start | bytes 52
  0.7 2.0 %copy-start.12 = (s32[1,1,4]{2,1,0:T(1,128)S(1)}, s32[1,1,4]{2,1,0:T(1,128)}, u32[]{:S(2)}) copy-start(s32[1,1,4]{2,1,0:T(1,128)} %param.12) | copy-start | bytes 52
  1.3 14.6 %copy-start = (f32[2,384,256]{2,1,0:T(8,128)S(1)}, f32[2,384,256]{2,1,0:T(8,128)}, u32[]{:S(2)}) copy-start(f32[2,384,256]{2,1,0:T(8,128)} %center.1) | copy-start | bytes 2359300
  2.8 13.2 %collective-permute-start.1 = (f32[2,392,128]{2,1,0:T(8,128)S(1)}, f32[2,392,128]{2,1,0:T(8,128)S(1)}, u32[]{:S(2)}, u32[]{:S(2)}) collective-permute-start(f32[2,392,128]{2,1,0:T(8,128)S(1)} %get-tuple-element.29), channel_id=1, source_target_pairs={{1,2},{3,4},{5,6},{7,8},{9,10},{11,12},{13,14},{2,1},{4,3},{6,5},{... | collective-permute-start | bytes 1204232 | tf_op jit(solution)/shard_map/ppermute | solution.py:297
  7.3 9.9 %collective-permute-start = (f32[2,392,128]{2,1,0:T(8,128)S(1)}, f32[2,392,128]{2,1,0:T(8,128)S(1)}, u32[]{:S(2)}, u32[]{:S(2)}) collective-permute-start(f32[2,392,128]{2,1,0:T(8,128)S(1)} %get-tuple-element.30), channel_id=1, source_target_pairs={{0,1},{2,3},{4,5},{6,7},{8,9},{10,11},{12,13},{14,15},{1,0},{3,2},... | collective-permute-start | bytes 1204232 | tf_op jit(solution)/shard_map/ppermute | solution.py:297
  17.2 0.8 copy-start.2
  18.0 3.0 %copy-start.9 = (bf16[1,1,4,256,256]{4,3,2,1,0:T(8,128)(2,1)S(1)}, bf16[1,1,4,256,256]{4,3,2,1,0:T(8,128)(2,1)}, u32[]{:S(2)}) copy-start(bf16[1,1,4,256,256]{4,3,2,1,0:T(8,128)(2,1)} %param.11) | copy-start | bytes 1572868
  18.0 3.0 %copy-start.10 = (bf16[256,256]{1,0:T(8,128)(2,1)S(1)}, bf16[256,256]{1,0:T(8,128)(2,1)}, u32[]{:S(2)}) copy-start(bf16[256,256]{1,0:T(8,128)(2,1)} %constant.76.clone.order) | copy-start | bytes 393220
  18.0 16.0 %copy-start.1 = (f32[2,256,256]{2,1,0:T(8,128)S(1)}, f32[2,256,256]{2,1,0:T(8,128)}, u32[]{:S(2)}) copy-start(f32[2,256,256]{2,1,0:T(8,128)} %probe.5) | copy-start | bytes 1572868
  18.0 16.0 %copy-start.3 = (f32[2,392,128]{2,1,0:T(8,128)S(1)}, f32[2,392,128]{2,1,0:T(8,128)}, u32[]{:S(2)}) copy-start(f32[2,392,128]{2,1,0:T(8,128)} %copy-done.2) | copy-start | bytes 1204228
  18.0 16.0 %copy-start.7 = (bf16[4,256,256]{2,1,0:T(8,128)(2,1)S(1)}, bf16[4,256,256]{2,1,0:T(8,128)(2,1)}, u32[]{:S(2)}) copy-start(bf16[4,256,256]{2,1,0:T(8,128)(2,1)} %constant.88.low) | copy-start | bytes 1572868
  18.1 16.0 %copy-start.8 = (bf16[4,256,256]{2,1,0:T(8,128)(2,1)S(1)}, bf16[4,256,256]{2,1,0:T(8,128)(2,1)}, u32[]{:S(2)}) copy-start(bf16[4,256,256]{2,1,0:T(8,128)(2,1)} %constant.85.high) | copy-start | bytes 1572868
  18.1 15.8 %collective-permute-start.2 = (f32[2,136,512]{2,1,0:T(8,128)S(1)}, f32[2,136,512]{2,1,0:T(8,128)S(1)}, u32[]{:S(2)}, u32[]{:S(2)}) collective-permute-start(f32[2,136,512]{2,1,0:T(8,128)S(1)} %broadcast_select_fusion.1), channel_id=1, source_target_pairs={{0,16},{32,48},{64,80},{96,112},{128,144},{160,176},{192,208},{224... | collective-permute-start | bytes 1671176 | tf_op jit(solution)/shard_map/ppermute | solution.py:297
  20.2 13.8 %collective-permute-start.3 = (f32[2,136,512]{2,1,0:T(8,128)S(1)}, f32[2,136,512]{2,1,0:T(8,128)S(1)}, u32[]{:S(2)}, u32[]{:S(2)}) collective-permute-start(f32[2,136,512]{2,1,0:T(8,128)S(1)} %broadcast_select_fusion), channel_id=1, source_target_pairs={{16,32},{48,64},{80,96},{112,128},{144,160},{176,192},{208,224},{2... | collective-permute-start | bytes 1671176 | tf_op jit(solution)/shard_map/ppermute | solution.py:297
  34.0 5.5 %copy-start.5 = (f32[2,136,512]{2,1,0:T(8,128)}, f32[2,136,512]{2,1,0:T(8,128)S(1)}, u32[]{:S(2)}) copy-start(f32[2,136,512]{2,1,0:T(8,128)S(1)} %collective-permute-done.2.row_a) | copy-start | bytes 1671172
  34.0 5.5 %copy-start.6 = (f32[2,136,512]{2,1,0:T(8,128)}, f32[2,136,512]{2,1,0:T(8,128)S(1)}, u32[]{:S(2)}) copy-start(f32[2,136,512]{2,1,0:T(8,128)S(1)} %collective-permute-done.3.row_b) | copy-start | bytes 1671172
  39.5 0.9 copy-start.4
  40.4 0.8 copy-start.14
  41.2 0.8 copy-start.15
  42.0 18.3 %all-to-all-start = ((f32[8,192,128]{2,1,0:T(8,128)}), f32[8,192,128]{2,1,0:T(8,128)}, u32[]{:S(2)}, u32[]{:S(2)}) async-start(f32[8,192,128]{2,1,0:T(8,128)} %copy-done.4), calls=%async_computation | async-start | bytes 1572864 | tf_op jit(solution)/shard_map/all_to_all | solution.py:314
  47.3 38.6 %collective-permute-start.4 = (f32[2,128,512]{2,1,0:T(8,128)}, f32[2,128,512]{2,1,0:T(8,128)}, u32[]{:S(2)}, u32[]{:S(2)}) collective-permute-start(f32[2,128,512]{2,1,0:T(8,128)} %copy-done.15), channel_id=1, source_target_pairs={{0,16},{32,48},{64,80},{96,112},{128,144},{160,176},{192,208},{224... | collective-permute-start | bytes 1572872 | tf_op jit(solution)/shard_map/ppermute | solution.py:297
  53.9 32.1 %collective-permute-start.5 = (f32[2,128,512]{2,1,0:T(8,128)}, f32[2,128,512]{2,1,0:T(8,128)}, u32[]{:S(2)}, u32[]{:S(2)}) collective-permute-start(f32[2,128,512]{2,1,0:T(8,128)} %copy-done.14), channel_id=1, source_target_pairs={{16,32},{48,64},{80,96},{112,128},{144,160},{176,192},{208,224},{2... | collective-permute-start | bytes 1572872 | tf_op jit(solution)/shard_map/ppermute | solution.py:297
  62.1 30.6 %all-to-all-start.1 = ((f32[8,24,128]{2,1,0:T(8,128)}), f32[8,24,128]{2,1,0:T(8,128)S(1)}, u32[]{:S(2)}, u32[]{:S(2)}) async-start(f32[8,24,128]{2,1,0:T(8,128)} %bitcast.14), calls=%async_computation.1 | async-start | bytes 196608 | tf_op jit(solution)/shard_map/all_to_all | solution.py:314
  93.7 47.1 %collective-permute-start.6 = (f32[2,384,128]{2,1,0:T(8,128)}, f32[2,384,128]{2,1,0:T(8,128)}, u32[]{:S(2)}, u32[]{:S(2)}) collective-permute-start(f32[2,384,128]{2,1,0:T(8,128)} %get-tuple-element.22), channel_id=1, source_target_pairs={{0,1},{2,3},{4,5},{6,7},{8,9},{10,11},{12,13},{14,15},{1,0},{3,2},... | collective-permute-start | bytes 1179656 | tf_op jit(solution)/shard_map/ppermute | solution.py:297
  97.1 43.6 %collective-permute-start.7 = (f32[2,384,128]{2,1,0:T(8,128)}, f32[2,384,128]{2,1,0:T(8,128)}, u32[]{:S(2)}, u32[]{:S(2)}) collective-permute-start(f32[2,384,128]{2,1,0:T(8,128)} %get-tuple-element.23), channel_id=1, source_target_pairs={{1,2},{3,4},{5,6},{7,8},{9,10},{11,12},{13,14},{2,1},{4,3},{6,5},{... | collective-permute-start | bytes 1179656 | tf_op jit(solution)/shard_map/ppermute | solution.py:297
  127.9 22.2 %all-to-all-start.5 = ((f32[8,128,128]{2,1,0:T(8,128)}), f32[8,128,128]{2,1,0:T(8,128)S(1)}, u32[]{:S(2)}, u32[]{:S(2)}) async-start(f32[8,128,128]{2,1,0:T(8,128)} %probe_piece.1), calls=%async_computation.5 | async-start | bytes 1048576 | tf_op jit(solution)/shard_map/all_to_all | solution.py:314

commit v5 on v4

--- a/solution.py
+++ b/solution.py
@@ -241,6 +241,26 @@
     )(pieces)
 
 
+def relay_kernel(parts, out):
+    total = parts[0]
+    for p in range(1, parts.shape[0]):
+        total = total + parts[p]
+    for p in range(out.shape[0]):
+        out[p] = total
+
+
+def relayed(parts, axes):
+    vmem = pl.BlockSpec(memory_space=pltpu.VMEM)
+    return pl.pallas_call(
+        relay_kernel,
+        in_specs=[vmem],
+        out_specs=vmem,
+        out_shape=jax.ShapeDtypeStruct((lax.axis_size(axes),) + parts.shape[1:], F32),
+        compiler_params=pltpu.CompilerParams(vmem_limit_bytes=SMALL_VMEM),
+        name="relay",
+    )(parts)
+
+
 def light_kernel(scans_at, probe, share, lit):
     width = probe.shape[1]
     rim = width // 2
@@ -312,10 +332,6 @@
 
 def exchanged(array, axes):
     return lax.all_to_all(array.reshape(lax.axis_size(axes), -1, array.shape[-1]), axes, 0, 0, tiled=True)
-
-
-def copied(array, axes):
-    return jnp.broadcast_to(array[None], (lax.axis_size(axes),) + array.shape)
 
 
 def halo(object_field, note):
@@ -382,11 +398,10 @@
     grad = row_folded(grad, above, below)
     mine = exchanged(mine, MID)
     grad, mine = lax.optimization_barrier((grad, mine))
-    mine = mine.sum(0)
     grad = col_folded(grad, rim)
-    mine = exchanged(copied(mine, ("z_lo",)), ("z_lo",)).sum(0)
-    mine = exchanged(copied(mine, ("z_hi",)), ("z_hi",)).sum(0)
-    mine = exchanged(copied(mine, MID), MID).reshape(-1, rim)
+    mine = exchanged(relayed(mine, ("z_lo",)), ("z_lo",))
+    mine = exchanged(relayed(mine, ("z_hi",)), ("z_hi",))
+    mine = exchanged(relayed(mine, MID), MID).reshape(-1, rim)
     mine = exchanged(probe_piece(mine, probe_field, near, lax.axis_index(NEAR)), NEAR)
     return object_field + grad * share, probe_joined(mine, probe_field)
 

time: 152 us -> 152 us (level)
    unnamed x32 -> x36, local copies, waits for them, and re-layouts: 3.26 us -> 3.26 us
where the time goes in v5:
time: 152 us; the launch traced here: 151 us
  starting transfers between devices  72.9 us (48%)
  blocking collectives  26.4 us (17%)
  waiting for transfers between devices  25.2 us (17%)
  Pallas kernels  11.8 us (8%)
  other arithmetic  8.35 us (5%)
  local copies, waits for them, and re-layouts  4.67 us (3%)
  between operations  1.73 us (1%)
    all_to_all x3, starting transfers between devices, exchanged(): lax.all_to_all(array.reshape(lax.axis_size(axes), -1, array.shape[-1]), a...  42 us
    ppermute x8, starting transfers between devices, swap(): return lax.ppermute(part, axis, pairs + [(j, i) for i, j in pairs])  30.9 us
    all_to_all x3, blocking collectives, exchanged(): lax.all_to_all(array.reshape(lax.axis_size(axes), -1, array.shape[-1]), a...  26.4 us
    ppermute x8, waiting for transfers between devices, swap(): return lax.ppermute(part, axis, pairs + [(j, i) for i, j in pairs])  12.9 us
    all_to_all x3, waiting for transfers between devices, exchanged(): lax.all_to_all(array.reshape(lax.axis_size(axes), -1, array.shape[-1]), a...  12.3 us
    pallas_call x1, Pallas kernels, scans(): pl.pallas_call(scan_kernel, in_specs=[smem] * 5 + [vmem] * 9, out_specs=[...  5.47 us
    pallas_call x1, Pallas kernels, light_share(): pl.pallas_call(light_kernel, in_specs=[pl.BlockSpec(memory_space=pltpu.SM...  3.42 us
    unnamed x36, local copies, waits for them, and re-layouts  3.26 us
  transfers between devices with their start and end apart: 11, of which 4 were waited for; matrix products, arithmetic and copies ran while one was open for 5% of the time, Pallas kernels for 4%

profile of v5, /device:TPU:1, one launch (start us, length us, event | category | flops | bytes accessed | tf_op | source)
XLA Modules:
  0.0 151.0 jit_solution(16404960969566369250)
XLA Ops:
  1.3 1.2 fusion.13
  2.6 0.1 add_convert_fusion
  2.7 0.1 fusion.3
  2.8 4.5 %collective-permute-start.1 = (f32[2,392,128]{2,1,0:T(8,128)S(1)}, f32[2,392,128]{2,1,0:T(8,128)S(1)}, u32[]{:S(2)}, u32[]{:S(2)}) collective-permute-start(f32[2,392,128]{2,1,0:T(8,128)S(1)} %get-tuple-element.29), channel_id=1, source_target_pairs={{1,2},{3,4},{5,6},{7,8},{9,10},{11,12},{13,14},{2,1},{4,3},{6,5},{... | collective-permute-start | bytes 1204232 | tf_op jit(solution)/shard_map/ppermute | solution.py:317
  7.3 8.6 %collective-permute-start = (f32[2,392,128]{2,1,0:T(8,128)S(1)}, f32[2,392,128]{2,1,0:T(8,128)S(1)}, u32[]{:S(2)}, u32[]{:S(2)}) collective-permute-start(f32[2,392,128]{2,1,0:T(8,128)S(1)} %get-tuple-element.30), channel_id=1, source_target_pairs={{0,1},{2,3},{4,5},{6,7},{8,9},{10,11},{12,13},{14,15},{1,0},{3,2},... | collective-permute-start | bytes 1204232 | tf_op jit(solution)/shard_map/ppermute | solution.py:317
  16.0 1.2 collective-permute-done.col_a
  17.2 0.7 copy-done.2
  17.9 0.1 broadcast_select_fusion
  18.0 0.0 copy-start.1
  18.0 0.0 copy-start.7
  18.0 0.0 copy-start.8
  18.1 0.1 broadcast_select_fusion.1
  18.1 2.1 %collective-permute-start.2 = (f32[2,136,512]{2,1,0:T(8,128)S(1)}, f32[2,136,512]{2,1,0:T(8,128)S(1)}, u32[]{:S(2)}, u32[]{:S(2)}) collective-permute-start(f32[2,136,512]{2,1,0:T(8,128)S(1)} %broadcast_select_fusion.1), channel_id=1, source_target_pairs={{0,16},{32,48},{64,80},{96,112},{128,144},{160,176},{192,208},{224... | collective-permute-start | bytes 1671176 | tf_op jit(solution)/shard_map/ppermute | solution.py:317
  20.2 0.7 collective-permute-start.3
  20.9 1.2 amplitude_order.1.amps
  22.2 0.1 and_select_fusion.odd
  22.3 11.7 %collective-permute-done.2.row_a = f32[2,136,512]{2,1,0:T(8,128)S(1)} collective-permute-done((f32[2,136,512]{2,1,0:T(8,128)S(1)}, f32[2,136,512]{2,1,0:T(8,128)S(1)}, u32[]{:S(2)}, u32[]{:S(2)}) %collective-permute-start.2) | collective-permute-done | bytes 557088 | tf_op jit(solution)/shard_map/ppermute | solution.py:317
  34.0 5.5 %scan_step.1 = (f32[2,128,512]{2,1,0:T(8,128)S(1)}, f32[2,384,512]{2,1,0:T(8,128)S(1)}, f32[2,128,512]{2,1,0:T(8,128)S(1)}, f32[8,192,128]{2,1,0:T(8,128)S(1)}) custom-call(s32[2]{0:T(128)S(1)} %bitcast.29, s32[4]{0:T(128)S(1)} %bitcast.31, s32[4]{0:T(128)S(1)} %bitcast.33, s32[1]{0:T(128)S(6)} %copy.11.count, s32[2]{0:T(128)S(1)} %and_select_fusion.odd, ...), custom_call_target="tpu_custom_call" | custom-call | tf_op jit(solution)/shard_map/scan_step/pallas_call | solution.py:182
  39.5 0.0 copy-start.4
  39.5 0.9 copy-done.4
  40.4 0.8 copy-done.14
  41.2 0.8 copy-done.15
  42.0 5.3 %all-to-all-start = ((f32[8,192,128]{2,1,0:T(8,128)}), f32[8,192,128]{2,1,0:T(8,128)}, u32[]{:S(2)}, u32[]{:S(2)}) async-start(f32[8,192,128]{2,1,0:T(8,128)} %copy-done.4), calls=%async_computation | async-start | bytes 1572864 | tf_op jit(solution)/shard_map/all_to_all | solution.py:334
  47.3 6.6 %collective-permute-start.4 = (f32[2,128,512]{2,1,0:T(8,128)}, f32[2,128,512]{2,1,0:T(8,128)}, u32[]{:S(2)}, u32[]{:S(2)}) collective-permute-start(f32[2,128,512]{2,1,0:T(8,128)} %copy-done.15), channel_id=1, source_target_pairs={{0,16},{32,48},{64,80},{96,112},{128,144},{160,176},{192,208},{224... | collective-permute-start | bytes 1572872 | tf_op jit(solution)/shard_map/ppermute | solution.py:317
  53.9 1.5 collective-permute-start.5
  55.3 0.7 fusion.8
  56.0 0.7 broadcast_select_fusion.2
  56.8 0.1 concatenate.43
  56.9 3.4 %light_share.1 = f32[384,256]{1,0:T(8,128)S(1)} custom-call(s32[99]{0:T(128)S(1)} %convert_element_type.21.scans_at, f32[2,256,256]{2,1,0:T(8,128)S(1)} %copy-done.1), custom_call_target="tpu_custom_call" | custom-call | flops 20000000 | bytes 1000000 | tf_op jit(solution)/shard_map/light_share/pallas_call | solution.py:293
  60.3 0.0 all-to-all-done
  60.3 1.8 %reduce_sum.9 = f32[192,128]{1,0:T(8,128)} reduce(f32[8,192,128]{2,1,0:T(8,128)} %all-to-all-done, f32[]{:T(128)} %constant.75.clone.1), dimensions={0}, to_apply=%region_0.1 | reduce | flops 172032 | bytes 884740 | tf_op jit(solution)/shard_map/reduce_sum | solution.py:397
  62.1 23.8 %all-to-all-start.1 = ((f32[8,24,128]{2,1,0:T(8,128)}), f32[8,24,128]{2,1,0:T(8,128)S(1)}, u32[]{:S(2)}, u32[]{:S(2)}) async-start(f32[8,24,128]{2,1,0:T(8,128)} %bitcast.14), calls=%async_computation.1 | async-start | bytes 196608 | tf_op jit(solution)/shard_map/all_to_all | solution.py:334
  86.0 0.0 collective-permute-done.4
  86.0 1.5 select_add_fusion.1
  87.5 0.1 pad_maximum_fusion
  87.6 5.1 %all-to-all-done.1.parts = f32[8,24,128]{2,1,0:T(8,128)S(1)} async-done(((f32[8,24,128]{2,1,0:T(8,128)}), f32[8,24,128]{2,1,0:T(8,128)S(1)}, u32[]{:S(2)}, u32[]{:S(2)}) %all-to-all-start.1) | async-done | bytes 98336 | tf_op jit(solution)/shard_map/all_to_all | solution.py:334
  92.7 0.9 slice_select_fusion.1
  93.7 3.5 %collective-permute-start.6 = (f32[2,384,128]{2,1,0:T(8,128)}, f32[2,384,128]{2,1,0:T(8,128)}, u32[]{:S(2)}, u32[]{:S(2)}) collective-permute-start(f32[2,384,128]{2,1,0:T(8,128)} %get-tuple-element.22), channel_id=1, source_target_pairs={{0,1},{2,3},{4,5},{6,7},{8,9},{10,11},{12,13},{14,15},{1,0},{3,2},... | collective-permute-start | bytes 1179656 | tf_op jit(solution)/shard_map/ppermute | solution.py:317
  97.1 3.6 %collective-permute-start.7 = (f32[2,384,128]{2,1,0:T(8,128)}, f32[2,384,128]{2,1,0:T(8,128)}, u32[]{:S(2)}, u32[]{:S(2)}) collective-permute-start(f32[2,384,128]{2,1,0:T(8,128)} %get-tuple-element.23), channel_id=1, source_target_pairs={{1,2},{3,4},{5,6},{7,8},{9,10},{11,12},{13,14},{2,1},{4,3},{6,5},{... | collective-permute-start | bytes 1179656 | tf_op jit(solution)/shard_map/ppermute | solution.py:317
  100.8 7.0 %all_to_all.30.parts = f32[4,24,128]{2,1,0:T(8,128)S(1)} all-to-all(f32[4,24,128]{2,1,0:T(8,128)S(1)} %relay.3), channel_id=1, replica_groups=mesh['y_lo'=4,'z_hi'=3,'z_lo'=4,'y_hi'=2,'x'=4,'core'=2] {'z_lo'}, dimensions={0} | all-to-all | bytes 98304 | tf_op jit(solution)/shard_map/all_to_all | solution.py:334
  107.8 10.2 %all_to_all.31.parts = f32[3,24,128]{2,1,0:T(8,128)S(1)} all-to-all(f32[3,24,128]{2,1,0:T(8,128)S(1)} %relay.4), channel_id=1, replica_groups=mesh['y_lo'=4,'z_hi'=3,'z_lo'=4,'y_hi'=2,'x'=4,'core'=2] {'z_hi'}, dimensions={0} | all-to-all | bytes 73728 | tf_op jit(solution)/shard_map/all_to_all | solution.py:334
  118.1 9.1 %all_to_all.32 = f32[8,24,128]{2,1,0:T(8,128)S(1)} all-to-all(f32[8,24,128]{2,1,0:T(8,128)S(1)} %relay.5), channel_id=1, replica_groups=mesh['y_lo'=4,'z_hi'=3,'z_lo'=4,'y_hi'=2,'x'=4,'core'=2] {'y_lo','y_hi'}, dimensions={0} | all-to-all | bytes 196608 | tf_op jit(solution)/shard_map/all_to_all | solution.py:334
  127.2 0.9 probe_piece.1
  128.0 12.8 %all-to-all-start.5 = ((f32[8,128,128]{2,1,0:T(8,128)}), f32[8,128,128]{2,1,0:T(8,128)S(1)}, u32[]{:S(2)}, u32[]{:S(2)}) async-start(f32[8,128,128]{2,1,0:T(8,128)} %probe_piece.1), calls=%async_computation.5 | async-start | bytes 1048576 | tf_op jit(solution)/shard_map/all_to_all | solution.py:334
  140.9 1.2 select_add_fusion.3
  142.1 1.0 fusion
  143.0 7.2 %all-to-all-done.5.pieces = f32[8,128,128]{2,1,0:T(8,128)S(1)} async-done(((f32[8,128,128]{2,1,0:T(8,128)}), f32[8,128,128]{2,1,0:T(8,128)S(1)}, u32[]{:S(2)}, u32[]{:S(2)}) %all-to-all-start.5) | async-done | bytes 524320 | tf_op jit(solution)/shard_map/all_to_all | solution.py:334
  150.2 0.8 probe_join.1
  (45 shorter events, 0.2 us)
Async XLA Ops:
  0.6 2.0 %copy-start.11 = (s32[1,1,2]{2,1,0:T(1,128)S(1)}, s32[1,1,2]{2,1,0:T(1,128)}, u32[]{:S(2)}) copy-start(s32[1,1,2]{2,1,0:T(1,128)} %param.14) | copy-start | bytes 28
  0.6 2.0 %copy-start.13 = (s32[1,1,4]{2,1,0:T(1,128)S(1)}, s32[1,1,4]{2,1,0:T(1,128)}, u32[]{:S(2)}) copy-start(s32[1,1,4]{2,1,0:T(1,128)} %param.13) | copy-start | bytes 52
  0.7 2.0 %copy-start.12 = (s32[1,1,4]{2,1,0:T(1,128)S(1)}, s32[1,1,4]{2,1,0:T(1,128)}, u32[]{:S(2)}) copy-start(s32[1,1,4]{2,1,0:T(1,128)} %param.12) | copy-start | bytes 52
  1.3 14.6 %copy-start = (f32[2,384,256]{2,1,0:T(8,128)S(1)}, f32[2,384,256]{2,1,0:T(8,128)}, u32[]{:S(2)}) copy-start(f32[2,384,256]{2,1,0:T(8,128)} %center.1) | copy-start | bytes 2359300
  2.8 13.2 %collective-permute-start.1 = (f32[2,392,128]{2,1,0:T(8,128)S(1)}, f32[2,392,128]{2,1,0:T(8,128)S(1)}, u32[]{:S(2)}, u32[]{:S(2)}) collective-permute-start(f32[2,392,128]{2,1,0:T(8,128)S(1)} %get-tuple-element.29), channel_id=1, source_target_pairs={{1,2},{3,4},{5,6},{7,8},{9,10},{11,12},{13,14},{2,1},{4,3},{6,5},{... | collective-permute-start | bytes 1204232 | tf_op jit(solution)/shard_map/ppermute | solution.py:317
  7.3 9.9 %collective-permute-start = (f32[2,392,128]{2,1,0:T(8,128)S(1)}, f32[2,392,128]{2,1,0:T(8,128)S(1)}, u32[]{:S(2)}, u32[]{:S(2)}) collective-permute-start(f32[2,392,128]{2,1,0:T(8,128)S(1)} %get-tuple-element.30), channel_id=1, source_target_pairs={{0,1},{2,3},{4,5},{6,7},{8,9},{10,11},{12,13},{14,15},{1,0},{3,2},... | collective-permute-start | bytes 1204232 | tf_op jit(solution)/shard_map/ppermute | solution.py:317
  17.2 0.7 copy-start.2
  17.9 3.0 %copy-start.9 = (bf16[1,1,4,256,256]{4,3,2,1,0:T(8,128)(2,1)S(1)}, bf16[1,1,4,256,256]{4,3,2,1,0:T(8,128)(2,1)}, u32[]{:S(2)}) copy-start(bf16[1,1,4,256,256]{4,3,2,1,0:T(8,128)(2,1)} %param.11) | copy-start | bytes 1572868
  17.9 3.0 %copy-start.10 = (bf16[256,256]{1,0:T(8,128)(2,1)S(1)}, bf16[256,256]{1,0:T(8,128)(2,1)}, u32[]{:S(2)}) copy-start(bf16[256,256]{1,0:T(8,128)(2,1)} %constant.76.clone.order) | copy-start | bytes 393220
  18.0 16.0 %copy-start.1 = (f32[2,256,256]{2,1,0:T(8,128)S(1)}, f32[2,256,256]{2,1,0:T(8,128)}, u32[]{:S(2)}) copy-start(f32[2,256,256]{2,1,0:T(8,128)} %probe.5) | copy-start | bytes 1572868
  18.0 16.0 %copy-start.3 = (f32[2,392,128]{2,1,0:T(8,128)S(1)}, f32[2,392,128]{2,1,0:T(8,128)}, u32[]{:S(2)}) copy-start(f32[2,392,128]{2,1,0:T(8,128)} %copy-done.2) | copy-start | bytes 1204228
  18.0 16.0 %copy-start.7 = (bf16[4,256,256]{2,1,0:T(8,128)(2,1)S(1)}, bf16[4,256,256]{2,1,0:T(8,128)(2,1)}, u32[]{:S(2)}) copy-start(bf16[4,256,256]{2,1,0:T(8,128)(2,1)} %constant.88.low) | copy-start | bytes 1572868
  18.0 16.0 %copy-start.8 = (bf16[4,256,256]{2,1,0:T(8,128)(2,1)S(1)}, bf16[4,256,256]{2,1,0:T(8,128)(2,1)}, u32[]{:S(2)}) copy-start(bf16[4,256,256]{2,1,0:T(8,128)(2,1)} %constant.85.high) | copy-start | bytes 1572868
  18.1 15.8 %collective-permute-start.2 = (f32[2,136,512]{2,1,0:T(8,128)S(1)}, f32[2,136,512]{2,1,0:T(8,128)S(1)}, u32[]{:S(2)}, u32[]{:S(2)}) collective-permute-start(f32[2,136,512]{2,1,0:T(8,128)S(1)} %broadcast_select_fusion.1), channel_id=1, source_target_pairs={{0,16},{32,48},{64,80},{96,112},{128,144},{160,176},{192,208},{224... | collective-permute-start | bytes 1671176 | tf_op jit(solution)/shard_map/ppermute | solution.py:317
  20.2 13.8 %collective-permute-start.3 = (f32[2,136,512]{2,1,0:T(8,128)S(1)}, f32[2,136,512]{2,1,0:T(8,128)S(1)}, u32[]{:S(2)}, u32[]{:S(2)}) collective-permute-start(f32[2,136,512]{2,1,0:T(8,128)S(1)} %broadcast_select_fusion), channel_id=1, source_target_pairs={{16,32},{48,64},{80,96},{112,128},{144,160},{176,192},{208,224},{2... | collective-permute-start | bytes 1671176 | tf_op jit(solution)/shard_map/ppermute | solution.py:317
  34.0 5.5 %copy-start.5 = (f32[2,136,512]{2,1,0:T(8,128)}, f32[2,136,512]{2,1,0:T(8,128)S(1)}, u32[]{:S(2)}) copy-start(f32[2,136,512]{2,1,0:T(8,128)S(1)} %collective-permute-done.2.row_a) | copy-start | bytes 1671172
  34.0 5.5 %copy-start.6 = (f32[2,136,512]{2,1,0:T(8,128)}, f32[2,136,512]{2,1,0:T(8,128)S(1)}, u32[]{:S(2)}) copy-start(f32[2,136,512]{2,1,0:T(8,128)S(1)} %collective-permute-done.3.row_b) | copy-start | bytes 1671172
  39.5 0.9 copy-start.4
  40.4 0.8 copy-start.14
  41.2 0.8 copy-start.15
  42.0 18.3 %all-to-all-start = ((f32[8,192,128]{2,1,0:T(8,128)}), f32[8,192,128]{2,1,0:T(8,128)}, u32[]{:S(2)}, u32[]{:S(2)}) async-start(f32[8,192,128]{2,1,0:T(8,128)} %copy-done.4), calls=%async_computation | async-start | bytes 1572864 | tf_op jit(solution)/shard_map/all_to_all | solution.py:334
  47.3 38.7 %collective-permute-start.4 = (f32[2,128,512]{2,1,0:T(8,128)}, f32[2,128,512]{2,1,0:T(8,128)}, u32[]{:S(2)}, u32[]{:S(2)}) collective-permute-start(f32[2,128,512]{2,1,0:T(8,128)} %copy-done.15), channel_id=1, source_target_pairs={{0,16},{32,48},{64,80},{96,112},{128,144},{160,176},{192,208},{224... | collective-permute-start | bytes 1572872 | tf_op jit(solution)/shard_map/ppermute | solution.py:317
  53.9 32.1 %collective-permute-start.5 = (f32[2,128,512]{2,1,0:T(8,128)}, f32[2,128,512]{2,1,0:T(8,128)}, u32[]{:S(2)}, u32[]{:S(2)}) collective-permute-start(f32[2,128,512]{2,1,0:T(8,128)} %copy-done.14), channel_id=1, source_target_pairs={{16,32},{48,64},{80,96},{112,128},{144,160},{176,192},{208,224},{2... | collective-permute-start | bytes 1572872 | tf_op jit(solution)/shard_map/ppermute | solution.py:317
  62.1 30.6 %all-to-all-start.1 = ((f32[8,24,128]{2,1,0:T(8,128)}), f32[8,24,128]{2,1,0:T(8,128)S(1)}, u32[]{:S(2)}, u32[]{:S(2)}) async-start(f32[8,24,128]{2,1,0:T(8,128)} %bitcast.14), calls=%async_computation.1 | async-start | bytes 196608 | tf_op jit(solution)/shard_map/all_to_all | solution.py:334
  87.6 9.5 %copy-start.16 = (f32[2,384,512]{2,1,0:T(8,128)}, f32[2,384,512]{2,1,0:T(8,128)S(1)}, u32[]{:S(2)}) copy-start(f32[2,384,512]{2,1,0:T(8,128)S(1)} %pad_maximum_fusion) | copy-start | bytes 4718596
  93.7 47.2 %collective-permute-start.6 = (f32[2,384,128]{2,1,0:T(8,128)}, f32[2,384,128]{2,1,0:T(8,128)}, u32[]{:S(2)}, u32[]{:S(2)}) collective-permute-start(f32[2,384,128]{2,1,0:T(8,128)} %get-tuple-element.22), channel_id=1, source_target_pairs={{0,1},{2,3},{4,5},{6,7},{8,9},{10,11},{12,13},{14,15},{1,0},{3,2},... | collective-permute-start | bytes 1179656 | tf_op jit(solution)/shard_map/ppermute | solution.py:317
  97.1 43.7 %collective-permute-start.7 = (f32[2,384,128]{2,1,0:T(8,128)}, f32[2,384,128]{2,1,0:T(8,128)}, u32[]{:S(2)}, u32[]{:S(2)}) collective-permute-start(f32[2,384,128]{2,1,0:T(8,128)} %get-tuple-element.23), channel_id=1, source_target_pairs={{1,2},{3,4},{5,6},{7,8},{9,10},{11,12},{13,14},{2,1},{4,3},{6,5},{... | collective-permute-start | bytes 1179656 | tf_op jit(solution)/shard_map/ppermute | solution.py:317
  100.8 40.1 %copy-start.17 = (f32[2,384,512]{2,1,0:T(8,128)S(1)}, f32[2,384,512]{2,1,0:T(8,128)}, u32[]{:S(2)}) copy-start(f32[2,384,512]{2,1,0:T(8,128)} %copy-done.16) | copy-start | bytes 4718596
  128.0 22.2 %all-to-all-start.5 = ((f32[8,128,128]{2,1,0:T(8,128)}), f32[8,128,128]{2,1,0:T(8,128)S(1)}, u32[]{:S(2)}, u32[]{:S(2)}) async-start(f32[8,128,128]{2,1,0:T(8,128)} %probe_piece.1), calls=%async_computation.5 | async-start | bytes 1048576 | tf_op jit(solution)/shard_map/all_to_all | solution.py:334
